TPU v7x, 256 devices: a whole 4x4x8 slice. The times are simulated.
256 devices in a mesh: aa: 16 (over x_lo, y, core), ba: 16 (over z, x_hi).
Axes of the slice: x: 4 (x_hi: 2, x_lo: 2; x = x_hi * 2 + x_lo), y: 4, z: 8, core: 2. Of those that a mesh axis runs over, the one named last changes fastest.
Arguments:
- query: bfloat16 [6144, 4096], P('aa', 'ba'), may hold values from -28 to 28
- keys: bfloat16 [6144, 2048], P('aa', 'ba'), may hold values from -6 to 6
- values: bfloat16 [6144, 2048], P('aa', 'ba'), may hold values from -6 to 6
- grad_out: bfloat16 [6144, 5376], P('aa', 'ba'), may hold values from -6 to 6
- segment_ids: int32 [6144], P('aa'), may hold values from 0 to 5, never falling along the last dimension, each value on 1 to 3456 neighbouring positions
- w_query: bfloat16 [5376, 4096], P(None, 'ba'), may hold values from -0.125 to 0.125
- w_key: bfloat16 [5376, 2048], P(None, 'ba'), may hold values from -0.1875 to 0.1875
- w_value: bfloat16 [5376, 2048], P(None, 'ba'), may hold values from -0.1875 to 0.1875
- w_out: bfloat16 [4096, 5376], P('ba'), may hold values from -0.078125 to 0.078125
Outputs:
- grad_input: bfloat16 [6144, 5376], P('aa', 'ba')
Inputs may be any that keep to these rules, and one draw needn't show every extreme that they name: `segment_ids`: never falls along the sequence; each document has at most 3456 positions.
All inputs are finite; a program needn't handle non-finite values.
Results may differ from a plain program's by a relative error of at most 0.019.
Values may be sent and summed in bfloat16 or wider, within the bound.
No kernel may reach another device: no remote copies, remote signals or barrier semaphores. Data moves between devices by JAX's collectives and lax.ppermute only.
A program may use at most 128 MiB of HBM per device.

v0:
```python
import jax
import jax.numpy as jnp
from jax import lax
from jax.sharding import Mesh
from jax.sharding import PartitionSpec as P

D = 5376
HQ = 32
HD = 128
BA = ("ba_0", "ba_1")


NEG_FILL = -1e30


def sent_to_all(x, axis):
    copies = jnp.broadcast_to(x, (lax.axis_size(axis), *x.shape))
    return lax.all_to_all(copies, axis, split_axis=0, concat_axis=0, tiled=True)


def in_order(pieces, dim):
    pieces = jnp.moveaxis(pieces, 0, dim)
    dims = pieces.shape
    return pieces.reshape(*dims[:dim], dims[dim] * dims[dim + 1], *dims[dim + 2 :])


def collect(x, axis, dim):
    pieces = sent_to_all(x, axis)
    return in_order(pieces, dim)


def gathered_by_axis(x, axes, dim):
    result = x
    for number in range(len(axes) - 1, -1, -1):
        result = lax.all_gather(result, axes[number], axis=dim, tiled=True)
    return result


def sent_together(arrays, axis, dim, along):
    both = jnp.concatenate(arrays, axis=along)
    result, at, done = (lax.all_gather(both, axis, axis=dim, tiled=True), 0, [])
    for a in arrays:
        done.append(lax.slice_in_dim(result, at, at + a.shape[along], axis=along))
        at += a.shape[along]
    return tuple(done)


def from_behind(value, axis, steps):
    count = lax.axis_size(axis)
    pairs = [(source, (source + steps) % count) for source in range(count)]
    return lax.ppermute(value, axis, pairs)


def summed_rows(x, axes, dim):
    for axis in axes:
        x = lax.psum_scatter(x, axis, scatter_dimension=dim, tiled=True)
    return x


def block_scores(query, dout, keys, values, query_pos, query_seg, key_pos, key_seg, scaling):
    row_count = query.shape[0]
    col_count = keys.shape[0]
    groups = keys.shape[1] // HD
    query_four = query.reshape(row_count, groups, 2, HD)
    dout_four = dout.reshape(row_count, groups, 2, HD)
    key_three = keys.reshape(col_count, groups, HD)
    value_three = values.reshape(col_count, groups, HD)
    scores = (
        jnp.einsum("iagd,jad->agij", query_four, key_three, preferred_element_type=jnp.float32)
        * scaling
    )
    dprobs = jnp.einsum(
        "iagd,jad->agij", dout_four, value_three, preferred_element_type=jnp.float32
    )
    allowed = (key_pos[None, :] <= query_pos[:, None]) & (key_seg[None, :] == query_seg[:, None])
    return (scores, dprobs, allowed, query_four, dout_four, key_three)


def forward_stats(
    query, dout, keys, values, query_pos, query_seg, key_pos, key_seg, scaling, state
):
    run_max, run_sum, run_dot = state
    scores, dprobs, allowed, unused_q, unused_d, unused_k = block_scores(
        query, dout, keys, values, query_pos, query_seg, key_pos, key_seg, scaling
    )
    masked = jnp.where(allowed, scores, NEG_FILL)
    new_max = jnp.maximum(run_max, jnp.max(masked, axis=-1))
    expo = jnp.where(allowed, jnp.exp(scores - new_max[..., None]), 0.0)
    return (new_max, jnp.sum(expo, axis=-1), jnp.sum(expo * dprobs, axis=-1))


def block_grads(
    query, dout, row_lse, row_delta, keys, values, query_pos, query_seg, key_pos, key_seg, scaling
):
    scores, dprobs, allowed, query_four, dout_four, key_three = block_scores(
        query, dout, keys, values, query_pos, query_seg, key_pos, key_seg, scaling
    )
    softmax_w = jnp.where(allowed, jnp.exp(scores - row_lse[..., None]), 0.0)
    dscores = softmax_w * (dprobs - row_delta[..., None])
    softmax_low = softmax_w.astype(jnp.bfloat16)
    dscores_low = dscores.astype(jnp.bfloat16)
    grad_v = jnp.einsum(
        "agij,iagd->jad", softmax_low, dout_four, preferred_element_type=jnp.float32
    )
    grad_k = (
        jnp.einsum("agij,iagd->jad", dscores_low, query_four, preferred_element_type=jnp.float32)
        * scaling
    )
    grad_q = (
        jnp.einsum("agij,jad->iagd", dscores_low, key_three, preferred_element_type=jnp.float32)
        * scaling
    )
    return (
        grad_q.reshape(query.shape[0], -1),
        grad_k.reshape(keys.shape[0], -1),
        grad_v.reshape(keys.shape[0], -1),
    )


def project_back(grad, weight):
    return lax.dot_general(
        grad, weight, (((1,), (1,)), ((), ())), preferred_element_type=jnp.float32
    )


def local(query, keys, values, grad_out, segment_ids, w_query, w_key, w_value, w_out):
    seq_devices = lax.axis_size("aa")
    own_index = lax.axis_index("aa")
    tok_count = query.shape[0]
    scaling = (D / HQ) ** (-0.5)
    groups = keys.shape[1] // HD
    all_seg = collect(segment_ids, "aa", 0)
    dout = project_back(gathered_by_axis(grad_out, BA, 1), w_out).astype(jnp.bfloat16)
    offsets = lax.iota(jnp.int32, tok_count)
    own_pos = own_index * tok_count + offsets
    own_seg = lax.dynamic_slice_in_dim(all_seg, own_index * tok_count, tok_count)
    stat_shape = (groups, 2, tok_count)
    stats_start = (
        jnp.full(stat_shape, NEG_FILL, jnp.float32),
        jnp.zeros(stat_shape, jnp.float32),
        jnp.zeros(stat_shape, jnp.float32),
    )
    piece = sent_together((keys, values), "aa", 0, 1)
    width = piece[0].shape[0]
    key_pos = lax.iota(jnp.int32, width)
    key_seg = all_seg
    run_max, run_sum, run_dot = forward_stats(
        query, dout, piece[0], piece[1], own_pos, own_seg, key_pos, key_seg, scaling, stats_start
    )
    row_lse = run_max + jnp.log(run_sum)
    row_delta = run_dot / run_sum
    zero_q = jnp.zeros(query.shape, jnp.float32)
    zero_k = jnp.zeros(keys.shape, jnp.float32)

    def step_keys(step_index, state):
        (keys_now, values_now), (dk_now, dv_now), grad_q = state
        anchor = (own_index - step_index) % seq_devices
        key_pos = anchor * tok_count + offsets
        key_seg = lax.dynamic_slice_in_dim(all_seg, anchor * tok_count, tok_count)
        add_q, add_k, add_v = block_grads(
            query,
            dout,
            row_lse,
            row_delta,
            keys_now,
            values_now,
            own_pos,
            own_seg,
            key_pos,
            key_seg,
            scaling,
        )
        bundle_next = from_behind((keys_now, values_now), "aa", 1)
        sums_next = (
            from_behind((dk_now + add_k).astype(jnp.bfloat16), "aa", 1).astype(jnp.float32),
            from_behind((dv_now + add_v).astype(jnp.bfloat16), "aa", 1).astype(jnp.float32),
        )
        return (bundle_next, sums_next, grad_q + add_q)

    initial = ((keys, values), (zero_k, zero_k), zero_q)
    final = lax.fori_loop(0, seq_devices, step_keys, initial)
    grad_q = final[2]
    grad_k = final[1][0]
    grad_v = final[1][1]
    partial_value = (
        project_back(grad_q.astype(jnp.bfloat16), w_query)
        + project_back(grad_k.astype(jnp.bfloat16), w_key)
        + project_back(grad_v.astype(jnp.bfloat16), w_value)
    )
    return (
        summed_rows(partial_value.astype(jnp.bfloat16), BA, 1)
        .astype(jnp.float32)
        .astype(jnp.bfloat16)
    )


def solution(mesh):
    finer = Mesh(mesh.devices.reshape(mesh.shape["aa"], 8, 2), ("aa", "ba_0", "ba_1"))
    return jax.shard_map(
        local,
        mesh=finer,
        in_specs=(
            P("aa", BA),
            P("aa", BA),
            P("aa", BA),
            P("aa", BA),
            P("aa"),
            P(None, BA),
            P(None, BA),
            P(None, BA),
            P(BA, None),
        ),
        out_specs=P("aa", BA),
        check_vma=False,
    )
```

profile of v0, /device:TPU:24, one launch (start us, length us, event | category | flops | bytes accessed | tf_op | source)
XLA Modules:
  0.0 455.0 jit_solution(4350359861143738034)
XLA Ops:
  6.5 1.7 copy.76
  8.2 1.6 pad_maximum_fusion
  9.9 11.9 %all_gather.10 = bf16[384,672]{0,1:T(8,128)(2,1)} all-gather(bf16[384,336]{0,1:T(8,128)(2,1)} %param.14), channel_id=1, replica_groups=mesh['aa'=16,'ba_0'=8,'ba_1'=2] {'ba_1'}, dimensions={1}, use_global_device_ids=true | all-gather | bytes 774144 | tf_op jit(solution)/shard_map/all_gather | solution.py:35
  23.2 4.7 %all-to-all-start = ((s32[16,1,384]{2,1,0:T(1,128)}), s32[16,1,384]{2,1,0:T(1,128)S(1)}, u32[]{:S(2)}, u32[]{:S(2)}) async-start(s32[16,1,384]{2,1,0:T(1,128)} %broadcast_in_dim.70), calls=%async_computation | async-start | bytes 49152 | tf_op jit(solution)/shard_map/all_to_all | solution.py:18
  27.9 1.6 copy.18
  29.6 2.5 all-to-all-done
  32.1 3.8 fusion.35
  35.9 13.8 %all-gather.3.cloned.1.call-done = bf16[6144,256]{1,0:T(8,128)(2,1)} async-done(((bf16[384,256]{1,0:T(8,128)(2,1)}), bf16[6144,256]{1,0:T(8,128)(2,1)}) %all-gather.3.cloned.1.call-update) | async-done | bytes 3145744 | tf_op jit(solution)/shard_map/all_gather | solution.py:41
  49.8 5.3 %fusion.31 = (f32[2,384]{1,0:T(2,128)S(1)}, f32[6144,384,2]{1,0,2:T(8,128)S(1)}) fusion(pred[384,6144]{0,1:T(8,128)(4,1)} %fusion.35, bf16[6144,256]{1,0:T(8,128)(2,1)} %all-gather.3.cloned.1.call-done, bf16[384,256]{1,0:T(8,128)(2,1)S(1)} %copy-done.6), kind=kOutput, calls=%fused_computation.41 | convolution fusion | flops 1222114560 | bytes 23006208 | tf_op jit(solution)/shard_map/iagd,jad->agij/dot_general | solution.py:69
  55.7 5.9 %copy-done.1 = f32[6144,384,2]{1,0,2:T(8,128)} copy-done((f32[6144,384,2]{1,0,2:T(8,128)}, f32[6144,384,2]{1,0,2:T(8,128)S(1)}, u32[]{:S(2)}) %copy-start.1) | copy-done | bytes 18874392
  61.6 5.8 %fusion.34 = f32[2,384]{1,0:T(2,128)S(1)} fusion(f32[6144,384,2]{1,0,2:T(8,128)S(1)} %get-tuple-element.458, f32[2,384]{1,0:T(2,128)S(1)} %broadcast_maximum_fusion, pred[384,6144]{0,1:T(8,128)(4,1)} %fusion.35), kind=kLoop, calls=%fused_computation.44 | loop fusion | flops 18873600 | bytes 21239808 | tf_op jit(solution)/shard_map/reduce_sum | solution.py:89
  67.4 39.3 %all-gather.5.cloned.1.call-done = bf16[384,5376]{0,1:T(8,128)(2,1)} async-done(((bf16[384,672]{0,1:T(8,128)(2,1)}), bf16[384,5376]{0,1:T(8,128)(2,1)}) %all-gather.5.cloned.1.call-update) | async-done | bytes 4128784 | tf_op jit(solution)/shard_map/all_gather | solution.py:35
  106.7 4.6 %convolution_convert_fusion = bf16[384,256]{0,1:T(8,128)(2,1)S(1)} fusion(bf16[256,5376]{1,0:T(8,128)(2,1)} %param.19, bf16[384,5376]{0,1:T(8,128)(2,1)} %all-gather.5.cloned.1.call-done), kind=kOutput, calls=%fused_computation.53 | convolution fusion | flops 1057062912 | bytes 7077888 | tf_op jit(solution)/shard_map/dot_general | solution.py:121
  111.5 10.4 %fusion.30 = f32[2,384]{1,0:T(2,128)S(1)} fusion(f32[6144,384,2]{1,0,2:T(8,128)} %copy-done.1, bf16[384,2,128]{0,2,1:T(8,128)(2,1)S(1)} %bitcast.180, f32[2,384]{1,0:T(2,128)S(1)} %broadcast_maximum_fusion, pred[384,6144]{0,1:T(8,128)(4,1)} %fusion.35, bf16[6144,256]{1,0:T(8,128)(2,1)} %all-gather.3.cloned.1.call-done), kind=kOutput, calls=%fused_computation.38 | convolution fusion | flops 1231551744 | bytes 23009280 | tf_op jit(solution)/shard_map/iagd,jad->agij/dot_general | solution.py:72
  122.5 244.6 %while.24 = (s32[]{:T(128)}, bf16[384,128]{0,1:T(8,128)(2,1)}, bf16[384,128]{1,0:T(8,128)(2,1)}, f32[384,128]{1,0:T(8,128)}, f32[384,128]{1,0:T(8,128)}, /*index...) while((s32[]{:T(128)}, bf16[384,128]{0,1:T(8,128)(2,1)}, ...), condition=%wide.region_4.5_spmd.clone, body=%wide.region_3.4_spmd.clone.sunk | while | flops 380732160 | bytes 13781608 | solution.py:181
  135.5 1.6 convert_element_type.116
  138.9 3.7 collective-permute-start
  147.7 3.0 collective-permute-done.2
  152.3 1.6 convert_element_type.116
  155.7 2.1 collective-permute-start
  162.9 3.0 collective-permute-done.2
  167.5 1.6 convert_element_type.116
  170.9 2.1 collective-permute-start
  178.1 3.0 collective-permute-done.2
  182.7 1.6 convert_element_type.116
  186.1 2.1 collective-permute-start
  193.4 3.0 collective-permute-done.2
  198.0 1.6 convert_element_type.116
  201.4 2.1 collective-permute-start
  208.6 3.0 collective-permute-done.2
  213.2 1.6 convert_element_type.116
  216.6 2.1 collective-permute-start
  223.8 3.0 collective-permute-done.2
  228.4 1.6 convert_element_type.116
  231.8 2.1 collective-permute-start
  239.1 3.0 collective-permute-done.2
  243.6 1.6 convert_element_type.116
  247.0 2.2 collective-permute-start
  254.3 3.0 collective-permute-done.2
  258.9 1.6 convert_element_type.116
  262.3 2.2 collective-permute-start
  269.5 3.0 collective-permute-done.2
  274.1 1.6 convert_element_type.116
  277.5 2.1 collective-permute-start
  284.7 3.0 collective-permute-done.2
  289.3 1.6 convert_element_type.116
  292.7 2.1 collective-permute-start
  300.0 3.0 collective-permute-done.2
  304.5 1.6 convert_element_type.116
  307.9 2.1 collective-permute-start
  315.2 3.0 collective-permute-done.2
  319.8 1.6 convert_element_type.116
  323.2 2.1 collective-permute-start
  330.4 3.0 collective-permute-done.2
  335.0 1.6 convert_element_type.116
  338.4 2.1 collective-permute-start
  345.6 3.0 collective-permute-done.2
  350.2 1.6 convert_element_type.116
  353.6 2.1 collective-permute-start
  360.9 3.0 collective-permute-done.2
  367.1 1.6 fusion.40
  370.2 3.2 fusion.36
  373.4 52.8 %reduce-scatter.3.cloned.1.call-done = bf16[384,672]{0,1:T(8,128)(2,1)} async-done(((bf16[384,5376]{0,1:T(8,128)(2,1)}), bf16[384,672]{0,1:T(8,128)(2,1)}) %reduce-scatter.3.cloned.1.call-update) | async-done | bytes 516112 | tf_op jit(solution)/shard_map/reduce_scatter | solution.py:56
  426.3 22.1 %reduce-scatter.5.cloned.1.call-done = bf16[384,336]{0,1:T(8,128)(2,1)} async-done(((bf16[384,672]{0,1:T(8,128)(2,1)}), bf16[384,336]{0,1:T(8,128)(2,1)}) %reduce-scatter.5.cloned.1.call-update) | async-done | bytes 258064 | tf_op jit(solution)/shard_map/reduce_scatter | solution.py:56
  (440 shorter events, 145.1 us)
Async XLA Ops:
  6.5 43.2 %all-gather.3.cloned.1.call-start = ((), (), s32[]{:S(2)}) async-start(), calls=%async_computation.3 | async-start | bytes 3342336 | tf_op jit(solution)/shard_map/all_gather | solution.py:41
  9.9 96.8 %all-gather.5.cloned.1.call-start = ((), (), s32[]{:S(2)}) async-start(), calls=%async_computation.4 | async-start | bytes 4644864 | tf_op jit(solution)/shard_map/all_gather | solution.py:35
  23.2 8.9 %all-to-all-start = ((s32[16,1,384]{2,1,0:T(1,128)}), s32[16,1,384]{2,1,0:T(1,128)S(1)}, u32[]{:S(2)}, u32[]{:S(2)}) async-start(s32[16,1,384]{2,1,0:T(1,128)} %broadcast_in_dim.70), calls=%async_computation | async-start | bytes 49152 | tf_op jit(solution)/shard_map/all_to_all | solution.py:18
  27.9 398.4 %reduce-scatter.3.cloned.1.call-start = ((), (), s32[]{:S(2)}) async-start(), calls=%async_computation.5 | async-start | bytes 4644864 | tf_op jit(solution)/shard_map/reduce_scatter | solution.py:56
  123.4 13.7 %collective-permute-start.1 = (bf16[384,128]{1,0:T(8,128)(2,1)S(1)}, bf16[384,128]{1,0:T(8,128)(2,1)}, u32[]{:S(2)}, u32[]{:S(2)}) collective-permute-start(bf16[384,128]{1,0:T(8,128)(2,1)S(1)} %copy.65), channel_id=1, source_target_pairs={{0,16},{16,32},{32,48},{48,64},{64,80},{80,96},{96,112},{112,128},... | collective-permute-start | bytes 294920 | tf_op jit(solution)/shard_map/while/body/eval_jaxpr/ppermute | solution.py:51
  124.3 12.8 %collective-permute-start = (bf16[384,128]{0,1:T(8,128)(2,1)S(1)}, bf16[384,128]{0,1:T(8,128)(2,1)}, u32[]{:S(2)}, u32[]{:S(2)}) collective-permute-start(bf16[384,128]{0,1:T(8,128)(2,1)S(1)} %copy.64), channel_id=1, source_target_pairs={{0,16},{16,32},{32,48},{48,64},{64,80},{80,96},{96,112},{112,128},... | collective-permute-start | bytes 294920 | tf_op jit(solution)/shard_map/while/body/eval_jaxpr/ppermute | solution.py:51
  130.5 5.0 %collective-permute-start.3 = (bf16[384,128]{1,0:T(8,128)(2,1)}, bf16[384,128]{1,0:T(8,128)(2,1)}, u32[]{:S(2)}, u32[]{:S(2)}) collective-permute-start(bf16[384,128]{1,0:T(8,128)(2,1)} %fusion.92), channel_id=1, source_target_pairs={{0,16},{16,32},{32,48},{48,64},{64,80},{80,96},{96,112},{112,128},... | collective-permute-start | bytes 294920 | tf_op jit(solution)/shard_map/while/body/eval_jaxpr/ppermute | solution.py:51
  138.0 15.9 %collective-permute-start.1 = (bf16[384,128]{1,0:T(8,128)(2,1)S(1)}, bf16[384,128]{1,0:T(8,128)(2,1)}, u32[]{:S(2)}, u32[]{:S(2)}) collective-permute-start(bf16[384,128]{1,0:T(8,128)(2,1)S(1)} %copy.65), channel_id=1, source_target_pairs={{0,16},{16,32},{32,48},{48,64},{64,80},{80,96},{96,112},{112,128},... | collective-permute-start | bytes 294920 | tf_op jit(solution)/shard_map/while/body/eval_jaxpr/ppermute | solution.py:51
  138.9 15.0 %collective-permute-start = (bf16[384,128]{0,1:T(8,128)(2,1)S(1)}, bf16[384,128]{0,1:T(8,128)(2,1)}, u32[]{:S(2)}, u32[]{:S(2)}) collective-permute-start(bf16[384,128]{0,1:T(8,128)(2,1)S(1)} %copy.64), channel_id=1, source_target_pairs={{0,16},{16,32},{32,48},{48,64},{64,80},{80,96},{96,112},{112,128},... | collective-permute-start | bytes 294920 | tf_op jit(solution)/shard_map/while/body/eval_jaxpr/ppermute | solution.py:51
  146.3 4.4 collective-permute-start.2
  147.3 5.0 %collective-permute-start.3 = (bf16[384,128]{1,0:T(8,128)(2,1)}, bf16[384,128]{1,0:T(8,128)(2,1)}, u32[]{:S(2)}, u32[]{:S(2)}) collective-permute-start(bf16[384,128]{1,0:T(8,128)(2,1)} %fusion.92), channel_id=1, source_target_pairs={{0,16},{16,32},{32,48},{48,64},{64,80},{80,96},{96,112},{112,128},... | collective-permute-start | bytes 294920 | tf_op jit(solution)/shard_map/while/body/eval_jaxpr/ppermute | solution.py:51
  154.8 14.3 %collective-permute-start.1 = (bf16[384,128]{1,0:T(8,128)(2,1)S(1)}, bf16[384,128]{1,0:T(8,128)(2,1)}, u32[]{:S(2)}, u32[]{:S(2)}) collective-permute-start(bf16[384,128]{1,0:T(8,128)(2,1)S(1)} %copy.65), channel_id=1, source_target_pairs={{0,16},{16,32},{32,48},{48,64},{64,80},{80,96},{96,112},{112,128},... | collective-permute-start | bytes 294920 | tf_op jit(solution)/shard_map/while/body/eval_jaxpr/ppermute | solution.py:51
  155.7 13.4 %collective-permute-start = (bf16[384,128]{0,1:T(8,128)(2,1)S(1)}, bf16[384,128]{0,1:T(8,128)(2,1)}, u32[]{:S(2)}, u32[]{:S(2)}) collective-permute-start(bf16[384,128]{0,1:T(8,128)(2,1)S(1)} %copy.64), channel_id=1, source_target_pairs={{0,16},{16,32},{32,48},{48,64},{64,80},{80,96},{96,112},{112,128},... | collective-permute-start | bytes 294920 | tf_op jit(solution)/shard_map/while/body/eval_jaxpr/ppermute | solution.py:51
  161.6 4.4 collective-permute-start.2
  162.6 5.0 %collective-permute-start.3 = (bf16[384,128]{1,0:T(8,128)(2,1)}, bf16[384,128]{1,0:T(8,128)(2,1)}, u32[]{:S(2)}, u32[]{:S(2)}) collective-permute-start(bf16[384,128]{1,0:T(8,128)(2,1)} %fusion.92), channel_id=1, source_target_pairs={{0,16},{16,32},{32,48},{48,64},{64,80},{80,96},{96,112},{112,128},... | collective-permute-start | bytes 294920 | tf_op jit(solution)/shard_map/while/body/eval_jaxpr/ppermute | solution.py:51
  170.0 14.3 %collective-permute-start.1 = (bf16[384,128]{1,0:T(8,128)(2,1)S(1)}, bf16[384,128]{1,0:T(8,128)(2,1)}, u32[]{:S(2)}, u32[]{:S(2)}) collective-permute-start(bf16[384,128]{1,0:T(8,128)(2,1)S(1)} %copy.65), channel_id=1, source_target_pairs={{0,16},{16,32},{32,48},{48,64},{64,80},{80,96},{96,112},{112,128},... | collective-permute-start | bytes 294920 | tf_op jit(solution)/shard_map/while/body/eval_jaxpr/ppermute | solution.py:51
  170.9 13.4 %collective-permute-start = (bf16[384,128]{0,1:T(8,128)(2,1)S(1)}, bf16[384,128]{0,1:T(8,128)(2,1)}, u32[]{:S(2)}, u32[]{:S(2)}) collective-permute-start(bf16[384,128]{0,1:T(8,128)(2,1)S(1)} %copy.64), channel_id=1, source_target_pairs={{0,16},{16,32},{32,48},{48,64},{64,80},{80,96},{96,112},{112,128},... | collective-permute-start | bytes 294920 | tf_op jit(solution)/shard_map/while/body/eval_jaxpr/ppermute | solution.py:51
  177.8 5.0 %collective-permute-start.3 = (bf16[384,128]{1,0:T(8,128)(2,1)}, bf16[384,128]{1,0:T(8,128)(2,1)}, u32[]{:S(2)}, u32[]{:S(2)}) collective-permute-start(bf16[384,128]{1,0:T(8,128)(2,1)} %fusion.92), channel_id=1, source_target_pairs={{0,16},{16,32},{32,48},{48,64},{64,80},{80,96},{96,112},{112,128},... | collective-permute-start | bytes 294920 | tf_op jit(solution)/shard_map/while/body/eval_jaxpr/ppermute | solution.py:51
  185.2 14.3 %collective-permute-start.1 = (bf16[384,128]{1,0:T(8,128)(2,1)S(1)}, bf16[384,128]{1,0:T(8,128)(2,1)}, u32[]{:S(2)}, u32[]{:S(2)}) collective-permute-start(bf16[384,128]{1,0:T(8,128)(2,1)S(1)} %copy.65), channel_id=1, source_target_pairs={{0,16},{16,32},{32,48},{48,64},{64,80},{80,96},{96,112},{112,128},... | collective-permute-start | bytes 294920 | tf_op jit(solution)/shard_map/while/body/eval_jaxpr/ppermute | solution.py:51
  186.1 13.4 %collective-permute-start = (bf16[384,128]{0,1:T(8,128)(2,1)S(1)}, bf16[384,128]{0,1:T(8,128)(2,1)}, u32[]{:S(2)}, u32[]{:S(2)}) collective-permute-start(bf16[384,128]{0,1:T(8,128)(2,1)S(1)} %copy.64), channel_id=1, source_target_pairs={{0,16},{16,32},{32,48},{48,64},{64,80},{80,96},{96,112},{112,128},... | collective-permute-start | bytes 294920 | tf_op jit(solution)/shard_map/while/body/eval_jaxpr/ppermute | solution.py:51
  193.0 5.0 %collective-permute-start.3 = (bf16[384,128]{1,0:T(8,128)(2,1)}, bf16[384,128]{1,0:T(8,128)(2,1)}, u32[]{:S(2)}, u32[]{:S(2)}) collective-permute-start(bf16[384,128]{1,0:T(8,128)(2,1)} %fusion.92), channel_id=1, source_target_pairs={{0,16},{16,32},{32,48},{48,64},{64,80},{80,96},{96,112},{112,128},... | collective-permute-start | bytes 294920 | tf_op jit(solution)/shard_map/while/body/eval_jaxpr/ppermute | solution.py:51
  200.5 14.3 %collective-permute-start.1 = (bf16[384,128]{1,0:T(8,128)(2,1)S(1)}, bf16[384,128]{1,0:T(8,128)(2,1)}, u32[]{:S(2)}, u32[]{:S(2)}) collective-permute-start(bf16[384,128]{1,0:T(8,128)(2,1)S(1)} %copy.65), channel_id=1, source_target_pairs={{0,16},{16,32},{32,48},{48,64},{64,80},{80,96},{96,112},{112,128},... | collective-permute-start | bytes 294920 | tf_op jit(solution)/shard_map/while/body/eval_jaxpr/ppermute | solution.py:51
  201.4 13.4 %collective-permute-start = (bf16[384,128]{0,1:T(8,128)(2,1)S(1)}, bf16[384,128]{0,1:T(8,128)(2,1)}, u32[]{:S(2)}, u32[]{:S(2)}) collective-permute-start(bf16[384,128]{0,1:T(8,128)(2,1)S(1)} %copy.64), channel_id=1, source_target_pairs={{0,16},{16,32},{32,48},{48,64},{64,80},{80,96},{96,112},{112,128},... | collective-permute-start | bytes 294920 | tf_op jit(solution)/shard_map/while/body/eval_jaxpr/ppermute | solution.py:51
  207.3 4.4 collective-permute-start.2
  208.2 5.0 %collective-permute-start.3 = (bf16[384,128]{1,0:T(8,128)(2,1)}, bf16[384,128]{1,0:T(8,128)(2,1)}, u32[]{:S(2)}, u32[]{:S(2)}) collective-permute-start(bf16[384,128]{1,0:T(8,128)(2,1)} %fusion.92), channel_id=1, source_target_pairs={{0,16},{16,32},{32,48},{48,64},{64,80},{80,96},{96,112},{112,128},... | collective-permute-start | bytes 294920 | tf_op jit(solution)/shard_map/while/body/eval_jaxpr/ppermute | solution.py:51
  215.7 14.3 %collective-permute-start.1 = (bf16[384,128]{1,0:T(8,128)(2,1)S(1)}, bf16[384,128]{1,0:T(8,128)(2,1)}, u32[]{:S(2)}, u32[]{:S(2)}) collective-permute-start(bf16[384,128]{1,0:T(8,128)(2,1)S(1)} %copy.65), channel_id=1, source_target_pairs={{0,16},{16,32},{32,48},{48,64},{64,80},{80,96},{96,112},{112,128},... | collective-permute-start | bytes 294920 | tf_op jit(solution)/shard_map/while/body/eval_jaxpr/ppermute | solution.py:51
  216.6 13.4 %collective-permute-start = (bf16[384,128]{0,1:T(8,128)(2,1)S(1)}, bf16[384,128]{0,1:T(8,128)(2,1)}, u32[]{:S(2)}, u32[]{:S(2)}) collective-permute-start(bf16[384,128]{0,1:T(8,128)(2,1)S(1)} %copy.64), channel_id=1, source_target_pairs={{0,16},{16,32},{32,48},{48,64},{64,80},{80,96},{96,112},{112,128},... | collective-permute-start | bytes 294920 | tf_op jit(solution)/shard_map/while/body/eval_jaxpr/ppermute | solution.py:51
  222.5 4.4 collective-permute-start.2
  223.5 5.0 %collective-permute-start.3 = (bf16[384,128]{1,0:T(8,128)(2,1)}, bf16[384,128]{1,0:T(8,128)(2,1)}, u32[]{:S(2)}, u32[]{:S(2)}) collective-permute-start(bf16[384,128]{1,0:T(8,128)(2,1)} %fusion.92), channel_id=1, source_target_pairs={{0,16},{16,32},{32,48},{48,64},{64,80},{80,96},{96,112},{112,128},... | collective-permute-start | bytes 294920 | tf_op jit(solution)/shard_map/while/body/eval_jaxpr/ppermute | solution.py:51
  230.9 14.3 %collective-permute-start.1 = (bf16[384,128]{1,0:T(8,128)(2,1)S(1)}, bf16[384,128]{1,0:T(8,128)(2,1)}, u32[]{:S(2)}, u32[]{:S(2)}) collective-permute-start(bf16[384,128]{1,0:T(8,128)(2,1)S(1)} %copy.65), channel_id=1, source_target_pairs={{0,16},{16,32},{32,48},{48,64},{64,80},{80,96},{96,112},{112,128},... | collective-permute-start | bytes 294920 | tf_op jit(solution)/shard_map/while/body/eval_jaxpr/ppermute | solution.py:51
  231.8 13.4 %collective-permute-start = (bf16[384,128]{0,1:T(8,128)(2,1)S(1)}, bf16[384,128]{0,1:T(8,128)(2,1)}, u32[]{:S(2)}, u32[]{:S(2)}) collective-permute-start(bf16[384,128]{0,1:T(8,128)(2,1)S(1)} %copy.64), channel_id=1, source_target_pairs={{0,16},{16,32},{32,48},{48,64},{64,80},{80,96},{96,112},{112,128},... | collective-permute-start | bytes 294920 | tf_op jit(solution)/shard_map/while/body/eval_jaxpr/ppermute | solution.py:51
  238.7 4.9 %collective-permute-start.3 = (bf16[384,128]{1,0:T(8,128)(2,1)}, bf16[384,128]{1,0:T(8,128)(2,1)}, u32[]{:S(2)}, u32[]{:S(2)}) collective-permute-start(bf16[384,128]{1,0:T(8,128)(2,1)} %fusion.92), channel_id=1, source_target_pairs={{0,16},{16,32},{32,48},{48,64},{64,80},{80,96},{96,112},{112,128},... | collective-permute-start | bytes 294920 | tf_op jit(solution)/shard_map/while/body/eval_jaxpr/ppermute | solution.py:51
  246.1 14.3 %collective-permute-start.1 = (bf16[384,128]{1,0:T(8,128)(2,1)S(1)}, bf16[384,128]{1,0:T(8,128)(2,1)}, u32[]{:S(2)}, u32[]{:S(2)}) collective-permute-start(bf16[384,128]{1,0:T(8,128)(2,1)S(1)} %copy.65), channel_id=1, source_target_pairs={{0,16},{16,32},{32,48},{48,64},{64,80},{80,96},{96,112},{112,128},... | collective-permute-start | bytes 294920 | tf_op jit(solution)/shard_map/while/body/eval_jaxpr/ppermute | solution.py:51
  247.0 13.4 %collective-permute-start = (bf16[384,128]{0,1:T(8,128)(2,1)S(1)}, bf16[384,128]{0,1:T(8,128)(2,1)}, u32[]{:S(2)}, u32[]{:S(2)}) collective-permute-start(bf16[384,128]{0,1:T(8,128)(2,1)S(1)} %copy.64), channel_id=1, source_target_pairs={{0,16},{16,32},{32,48},{48,64},{64,80},{80,96},{96,112},{112,128},... | collective-permute-start | bytes 294920 | tf_op jit(solution)/shard_map/while/body/eval_jaxpr/ppermute | solution.py:51
  252.9 4.4 collective-permute-start.2
  253.9 5.0 %collective-permute-start.3 = (bf16[384,128]{1,0:T(8,128)(2,1)}, bf16[384,128]{1,0:T(8,128)(2,1)}, u32[]{:S(2)}, u32[]{:S(2)}) collective-permute-start(bf16[384,128]{1,0:T(8,128)(2,1)} %fusion.92), channel_id=1, source_target_pairs={{0,16},{16,32},{32,48},{48,64},{64,80},{80,96},{96,112},{112,128},... | collective-permute-start | bytes 294920 | tf_op jit(solution)/shard_map/while/body/eval_jaxpr/ppermute | solution.py:51
  261.4 14.4 %collective-permute-start.1 = (bf16[384,128]{1,0:T(8,128)(2,1)S(1)}, bf16[384,128]{1,0:T(8,128)(2,1)}, u32[]{:S(2)}, u32[]{:S(2)}) collective-permute-start(bf16[384,128]{1,0:T(8,128)(2,1)S(1)} %copy.65), channel_id=1, source_target_pairs={{0,16},{16,32},{32,48},{48,64},{64,80},{80,96},{96,112},{112,128},... | collective-permute-start | bytes 294920 | tf_op jit(solution)/shard_map/while/body/eval_jaxpr/ppermute | solution.py:51
  262.3 13.5 %collective-permute-start = (bf16[384,128]{0,1:T(8,128)(2,1)S(1)}, bf16[384,128]{0,1:T(8,128)(2,1)}, u32[]{:S(2)}, u32[]{:S(2)}) collective-permute-start(bf16[384,128]{0,1:T(8,128)(2,1)S(1)} %copy.64), channel_id=1, source_target_pairs={{0,16},{16,32},{32,48},{48,64},{64,80},{80,96},{96,112},{112,128},... | collective-permute-start | bytes 294920 | tf_op jit(solution)/shard_map/while/body/eval_jaxpr/ppermute | solution.py:51
  269.1 5.0 %collective-permute-start.3 = (bf16[384,128]{1,0:T(8,128)(2,1)}, bf16[384,128]{1,0:T(8,128)(2,1)}, u32[]{:S(2)}, u32[]{:S(2)}) collective-permute-start(bf16[384,128]{1,0:T(8,128)(2,1)} %fusion.92), channel_id=1, source_target_pairs={{0,16},{16,32},{32,48},{48,64},{64,80},{80,96},{96,112},{112,128},... | collective-permute-start | bytes 294920 | tf_op jit(solution)/shard_map/while/body/eval_jaxpr/ppermute | solution.py:51
  276.6 14.3 %collective-permute-start.1 = (bf16[384,128]{1,0:T(8,128)(2,1)S(1)}, bf16[384,128]{1,0:T(8,128)(2,1)}, u32[]{:S(2)}, u32[]{:S(2)}) collective-permute-start(bf16[384,128]{1,0:T(8,128)(2,1)S(1)} %copy.65), channel_id=1, source_target_pairs={{0,16},{16,32},{32,48},{48,64},{64,80},{80,96},{96,112},{112,128},... | collective-permute-start | bytes 294920 | tf_op jit(solution)/shard_map/while/body/eval_jaxpr/ppermute | solution.py:51
  277.5 13.4 %collective-permute-start = (bf16[384,128]{0,1:T(8,128)(2,1)S(1)}, bf16[384,128]{0,1:T(8,128)(2,1)}, u32[]{:S(2)}, u32[]{:S(2)}) collective-permute-start(bf16[384,128]{0,1:T(8,128)(2,1)S(1)} %copy.64), channel_id=1, source_target_pairs={{0,16},{16,32},{32,48},{48,64},{64,80},{80,96},{96,112},{112,128},... | collective-permute-start | bytes 294920 | tf_op jit(solution)/shard_map/while/body/eval_jaxpr/ppermute | solution.py:51
  283.4 4.4 collective-permute-start.2
  284.4 5.0 %collective-permute-start.3 = (bf16[384,128]{1,0:T(8,128)(2,1)}, bf16[384,128]{1,0:T(8,128)(2,1)}, u32[]{:S(2)}, u32[]{:S(2)}) collective-permute-start(bf16[384,128]{1,0:T(8,128)(2,1)} %fusion.92), channel_id=1, source_target_pairs={{0,16},{16,32},{32,48},{48,64},{64,80},{80,96},{96,112},{112,128},... | collective-permute-start | bytes 294920 | tf_op jit(solution)/shard_map/while/body/eval_jaxpr/ppermute | solution.py:51
  291.8 14.3 %collective-permute-start.1 = (bf16[384,128]{1,0:T(8,128)(2,1)S(1)}, bf16[384,128]{1,0:T(8,128)(2,1)}, u32[]{:S(2)}, u32[]{:S(2)}) collective-permute-start(bf16[384,128]{1,0:T(8,128)(2,1)S(1)} %copy.65), channel_id=1, source_target_pairs={{0,16},{16,32},{32,48},{48,64},{64,80},{80,96},{96,112},{112,128},... | collective-permute-start | bytes 294920 | tf_op jit(solution)/shard_map/while/body/eval_jaxpr/ppermute | solution.py:51
  292.7 13.4 %collective-permute-start = (bf16[384,128]{0,1:T(8,128)(2,1)S(1)}, bf16[384,128]{0,1:T(8,128)(2,1)}, u32[]{:S(2)}, u32[]{:S(2)}) collective-permute-start(bf16[384,128]{0,1:T(8,128)(2,1)S(1)} %copy.64), channel_id=1, source_target_pairs={{0,16},{16,32},{32,48},{48,64},{64,80},{80,96},{96,112},{112,128},... | collective-permute-start | bytes 294920 | tf_op jit(solution)/shard_map/while/body/eval_jaxpr/ppermute | solution.py:51
  298.6 4.4 collective-permute-start.2
  299.6 4.9 %collective-permute-start.3 = (bf16[384,128]{1,0:T(8,128)(2,1)}, bf16[384,128]{1,0:T(8,128)(2,1)}, u32[]{:S(2)}, u32[]{:S(2)}) collective-permute-start(bf16[384,128]{1,0:T(8,128)(2,1)} %fusion.92), channel_id=1, source_target_pairs={{0,16},{16,32},{32,48},{48,64},{64,80},{80,96},{96,112},{112,128},... | collective-permute-start | bytes 294920 | tf_op jit(solution)/shard_map/while/body/eval_jaxpr/ppermute | solution.py:51
  307.0 14.3 %collective-permute-start.1 = (bf16[384,128]{1,0:T(8,128)(2,1)S(1)}, bf16[384,128]{1,0:T(8,128)(2,1)}, u32[]{:S(2)}, u32[]{:S(2)}) collective-permute-start(bf16[384,128]{1,0:T(8,128)(2,1)S(1)} %copy.65), channel_id=1, source_target_pairs={{0,16},{16,32},{32,48},{48,64},{64,80},{80,96},{96,112},{112,128},... | collective-permute-start | bytes 294920 | tf_op jit(solution)/shard_map/while/body/eval_jaxpr/ppermute | solution.py:51
  307.9 13.4 %collective-permute-start = (bf16[384,128]{0,1:T(8,128)(2,1)S(1)}, bf16[384,128]{0,1:T(8,128)(2,1)}, u32[]{:S(2)}, u32[]{:S(2)}) collective-permute-start(bf16[384,128]{0,1:T(8,128)(2,1)S(1)} %copy.64), channel_id=1, source_target_pairs={{0,16},{16,32},{32,48},{48,64},{64,80},{80,96},{96,112},{112,128},... | collective-permute-start | bytes 294920 | tf_op jit(solution)/shard_map/while/body/eval_jaxpr/ppermute | solution.py:51
  313.8 4.4 collective-permute-start.2
  314.8 5.0 %collective-permute-start.3 = (bf16[384,128]{1,0:T(8,128)(2,1)}, bf16[384,128]{1,0:T(8,128)(2,1)}, u32[]{:S(2)}, u32[]{:S(2)}) collective-permute-start(bf16[384,128]{1,0:T(8,128)(2,1)} %fusion.92), channel_id=1, source_target_pairs={{0,16},{16,32},{32,48},{48,64},{64,80},{80,96},{96,112},{112,128},... | collective-permute-start | bytes 294920 | tf_op jit(solution)/shard_map/while/body/eval_jaxpr/ppermute | solution.py:51
  322.3 14.3 %collective-permute-start.1 = (bf16[384,128]{1,0:T(8,128)(2,1)S(1)}, bf16[384,128]{1,0:T(8,128)(2,1)}, u32[]{:S(2)}, u32[]{:S(2)}) collective-permute-start(bf16[384,128]{1,0:T(8,128)(2,1)S(1)} %copy.65), channel_id=1, source_target_pairs={{0,16},{16,32},{32,48},{48,64},{64,80},{80,96},{96,112},{112,128},... | collective-permute-start | bytes 294920 | tf_op jit(solution)/shard_map/while/body/eval_jaxpr/ppermute | solution.py:51
  323.2 13.4 %collective-permute-start = (bf16[384,128]{0,1:T(8,128)(2,1)S(1)}, bf16[384,128]{0,1:T(8,128)(2,1)}, u32[]{:S(2)}, u32[]{:S(2)}) collective-permute-start(bf16[384,128]{0,1:T(8,128)(2,1)S(1)} %copy.64), channel_id=1, source_target_pairs={{0,16},{16,32},{32,48},{48,64},{64,80},{80,96},{96,112},{112,128},... | collective-permute-start | bytes 294920 | tf_op jit(solution)/shard_map/while/body/eval_jaxpr/ppermute | solution.py:51
  329.1 4.4 collective-permute-start.2
  330.1 5.0 %collective-permute-start.3 = (bf16[384,128]{1,0:T(8,128)(2,1)}, bf16[384,128]{1,0:T(8,128)(2,1)}, u32[]{:S(2)}, u32[]{:S(2)}) collective-permute-start(bf16[384,128]{1,0:T(8,128)(2,1)} %fusion.92), channel_id=1, source_target_pairs={{0,16},{16,32},{32,48},{48,64},{64,80},{80,96},{96,112},{112,128},... | collective-permute-start | bytes 294920 | tf_op jit(solution)/shard_map/while/body/eval_jaxpr/ppermute | solution.py:51
  337.5 14.3 %collective-permute-start.1 = (bf16[384,128]{1,0:T(8,128)(2,1)S(1)}, bf16[384,128]{1,0:T(8,128)(2,1)}, u32[]{:S(2)}, u32[]{:S(2)}) collective-permute-start(bf16[384,128]{1,0:T(8,128)(2,1)S(1)} %copy.65), channel_id=1, source_target_pairs={{0,16},{16,32},{32,48},{48,64},{64,80},{80,96},{96,112},{112,128},... | collective-permute-start | bytes 294920 | tf_op jit(solution)/shard_map/while/body/eval_jaxpr/ppermute | solution.py:51
  338.4 13.4 %collective-permute-start = (bf16[384,128]{0,1:T(8,128)(2,1)S(1)}, bf16[384,128]{0,1:T(8,128)(2,1)}, u32[]{:S(2)}, u32[]{:S(2)}) collective-permute-start(bf16[384,128]{0,1:T(8,128)(2,1)S(1)} %copy.64), channel_id=1, source_target_pairs={{0,16},{16,32},{32,48},{48,64},{64,80},{80,96},{96,112},{112,128},... | collective-permute-start | bytes 294920 | tf_op jit(solution)/shard_map/while/body/eval_jaxpr/ppermute | solution.py:51
  344.3 4.4 collective-permute-start.2
  345.3 5.0 %collective-permute-start.3 = (bf16[384,128]{1,0:T(8,128)(2,1)}, bf16[384,128]{1,0:T(8,128)(2,1)}, u32[]{:S(2)}, u32[]{:S(2)}) collective-permute-start(bf16[384,128]{1,0:T(8,128)(2,1)} %fusion.92), channel_id=1, source_target_pairs={{0,16},{16,32},{32,48},{48,64},{64,80},{80,96},{96,112},{112,128},... | collective-permute-start | bytes 294920 | tf_op jit(solution)/shard_map/while/body/eval_jaxpr/ppermute | solution.py:51
  352.7 14.3 %collective-permute-start.1 = (bf16[384,128]{1,0:T(8,128)(2,1)S(1)}, bf16[384,128]{1,0:T(8,128)(2,1)}, u32[]{:S(2)}, u32[]{:S(2)}) collective-permute-start(bf16[384,128]{1,0:T(8,128)(2,1)S(1)} %copy.65), channel_id=1, source_target_pairs={{0,16},{16,32},{32,48},{48,64},{64,80},{80,96},{96,112},{112,128},... | collective-permute-start | bytes 294920 | tf_op jit(solution)/shard_map/while/body/eval_jaxpr/ppermute | solution.py:51
  353.6 13.4 %collective-permute-start = (bf16[384,128]{0,1:T(8,128)(2,1)S(1)}, bf16[384,128]{0,1:T(8,128)(2,1)}, u32[]{:S(2)}, u32[]{:S(2)}) collective-permute-start(bf16[384,128]{0,1:T(8,128)(2,1)S(1)} %copy.64), channel_id=1, source_target_pairs={{0,16},{16,32},{32,48},{48,64},{64,80},{80,96},{96,112},{112,128},... | collective-permute-start | bytes 294920 | tf_op jit(solution)/shard_map/while/body/eval_jaxpr/ppermute | solution.py:51
  359.5 4.4 collective-permute-start.2
  360.5 5.0 %collective-permute-start.3 = (bf16[384,128]{1,0:T(8,128)(2,1)}, bf16[384,128]{1,0:T(8,128)(2,1)}, u32[]{:S(2)}, u32[]{:S(2)}) collective-permute-start(bf16[384,128]{1,0:T(8,128)(2,1)} %fusion.92), channel_id=1, source_target_pairs={{0,16},{16,32},{32,48},{48,64},{64,80},{80,96},{96,112},{112,128},... | collective-permute-start | bytes 294920 | tf_op jit(solution)/shard_map/while/body/eval_jaxpr/ppermute | solution.py:51
  373.4 75.1 %reduce-scatter.5.cloned.1.call-start = ((), (), s32[]{:S(2)}) async-start(), calls=%async_computation.6 | async-start | bytes 774144 | tf_op jit(solution)/shard_map/reduce_scatter | solution.py:56
  (63 other events, 621.1 us)
Sparse Core Ops, SparseCore 0:
  10.0 39.6 all-gather.2
  51.5 55.1 all-gather.4
  373.5 52.7 reduce-scatter.2
  428.6 19.7 reduce-scatter.4
where the time goes:
time: 459 us; the launch traced here: 455 us
  waiting for transfers between devices  177 us (39%)
  matrix products  88.6 us (19%)
  other arithmetic  66.9 us (15%)
  local copies, waits for them, and re-layouts  53.7 us (12%)
  starting transfers between devices  41.9 us (9%)
  between operations  13.3 us (3%)
  blocking collectives  11.9 us (3%)
    reduce_scatter x2, waiting for transfers between devices, summed_rows(): x = lax.psum_scatter(x, axis, scatter_dimension=dim, tiled=True)  75 us
    ppermute x64, waiting for transfers between devices, from_behind(): return lax.ppermute(value, axis, pairs)  46.8 us
    all_gather x1, waiting for transfers between devices, gathered_by_axis(): result = lax.all_gather(result, axes[number], axis=dim, tiled=True)  39.3 us
    ppermute x64, starting transfers between devices, from_behind(): return lax.ppermute(value, axis, pairs)  37 us
    while x128, local copies, waits for them, and re-layouts  28.8 us
    dot_general x17, matrix products, block_scores(): jnp.einsum('iagd,jad->agij', query_four, key_three, preferred_element_typ...  27.5 us
    convert_element_type x16, other arithmetic, step_keys(): from_behind((dv_now + add_v).astype(jnp.bfloat16), 'aa', 1)  25.4 us
    convert_element_type x16, other arithmetic, step_keys(): from_behind((dk_now + add_k).astype(jnp.bfloat16), 'aa', 1)  25.3 us
  transfers between devices with their start and end apart: 69, of which 21 were waited for; matrix products, arithmetic and copies ran while one was open for 36% of the time, Pallas kernels for 0%

commit v1 on v0

v1 whole, which is shorter than its diff:
```python
import math

import jax
import jax.numpy as jnp
from jax import lax
from jax.experimental import pallas as pl
from jax.experimental.pallas import tpu as pltpu
from jax.sharding import Mesh
from jax.sharding import PartitionSpec as P

D = 5376
HQ = 32
HD = 128
DOCS = 6
DOC_MOST = 3456
BA = ("ba_0", "ba_1")
NEG_FILL = -1e30
SCALE = (D / HQ) ** (-0.5)
SCALE2 = SCALE * math.log2(math.e)
F32 = jnp.float32
BF16 = jnp.bfloat16


def dot(a, b):
    return lax.dot_general(a, b, (((1,), (0,)), ((), ())), preferred_element_type=F32)


def row_limits(info, qseg_ref, rows):
    seg = qseg_ref[...]
    start = jnp.zeros((1, rows), jnp.int32)
    for s in range(DOCS):
        start = jnp.where(seg == s, info[2 + s], start)
    pos = info[1] + lax.broadcasted_iota(jnp.int32, (1, rows), 1)
    return start, pos


def stats_kernel(reach, info, qseg_ref, q_ref, *refs):
    kv_refs = refs[: reach + 1]
    lse_ref, out_ref, qt_ref, m_ref, l_ref = refs[reach + 1 :]
    rows = q_ref.shape[0]
    start, pos = row_limits(info, qseg_ref, rows)
    qt_ref[...] = q_ref[...].T
    m_ref[...] = jnp.full(m_ref.shape, NEG_FILL, F32)
    l_ref[...] = jnp.zeros(l_ref.shape, F32)
    out_ref[...] = jnp.zeros(out_ref.shape, F32)
    key_at = lax.broadcasted_iota(jnp.int32, (rows, rows), 0)
    for b in range(reach + 1):

        @pl.when(b >= info[0])
        def _(b=b):
            first = info[1] + (b - reach) * rows
            allowed = (key_at >= start - first) & (key_at <= pos - first)
            kb = kv_refs[b][:, :HD]
            vt = kv_refs[b][:, HD:].T
            for h in range(2):
                qt = qt_ref[h * HD : (h + 1) * HD, :]
                s = jnp.where(allowed, dot(kb, qt) * SCALE2, NEG_FILL)
                m_old = m_ref[h : h + 1, :]
                m_new = jnp.maximum(m_old, jnp.max(s, axis=0, keepdims=True))
                p = jnp.where(allowed, jnp.exp2(s - m_new), 0.0)
                back = jnp.exp2(m_old - m_new)
                l_ref[h : h + 1, :] = l_ref[h : h + 1, :] * back + jnp.sum(p, axis=0, keepdims=True)
                m_ref[h : h + 1, :] = m_new
                high = p.astype(BF16)
                low = (p - high.astype(F32)).astype(BF16)
                o = out_ref[h * HD : (h + 1) * HD, :]
                out_ref[h * HD : (h + 1) * HD, :] = o * back + (dot(vt, high) + dot(vt, low))

    lse_ref[...] = m_ref[...] + jnp.log2(l_ref[...])
    for h in range(2):
        out_ref[h * HD : (h + 1) * HD, :] = out_ref[h * HD : (h + 1) * HD, :] / l_ref[h : h + 1, :]


def grads_kernel(reach, info, qseg_ref, q_ref, doutt_ref, lse_ref, out_ref, *refs):
    kv_refs = refs[: reach + 1]
    gqt_ref = refs[reach + 1]
    gkv_refs = refs[reach + 2 : 2 * reach + 3]
    qt_ref, dout_ref, delta_ref, acc_ref = refs[2 * reach + 3 :]
    rows = q_ref.shape[0]
    start, pos = row_limits(info, qseg_ref, rows)
    qt_ref[...] = q_ref[...].T
    dout_ref[...] = doutt_ref[...].T
    for h in range(2):
        part = slice(h * HD, (h + 1) * HD)
        delta_ref[h : h + 1, :] = jnp.sum(
            doutt_ref[part, :].astype(F32) * out_ref[part, :], axis=0, keepdims=True
        )
    acc_ref[...] = jnp.zeros(acc_ref.shape, F32)
    key_at = lax.broadcasted_iota(jnp.int32, (rows, rows), 0)
    for b in range(reach + 1):

        @pl.when(b >= info[0])
        def _(b=b):
            first = info[1] + (b - reach) * rows
            allowed = (key_at >= start - first) & (key_at <= pos - first)
            kb = kv_refs[b][:, :HD]
            vb = kv_refs[b][:, HD:]
            kt = kb.T
            gk = gv = None
            for h in range(2):
                part = slice(h * HD, (h + 1) * HD)
                s = dot(kb, qt_ref[part, :]) * SCALE2
                dp = dot(vb, doutt_ref[part, :])
                p = jnp.where(allowed, jnp.exp2(s - lse_ref[h : h + 1, :]), 0.0)
                ds = (p * (dp - delta_ref[h : h + 1, :])).astype(BF16)
                add_v = dot(p.astype(BF16), dout_ref[:, part])
                add_k = dot(ds, q_ref[:, part])
                gv = add_v if h == 0 else gv + add_v
                gk = add_k if h == 0 else gk + add_k
                acc_ref[part, :] += dot(kt, ds)
            gkv_refs[b][:, :HD] = (gk * SCALE).astype(BF16)
            gkv_refs[b][:, HD:] = gv.astype(BF16)

        @pl.when(b < info[0])
        def _(b=b):
            gkv_refs[b][...] = jnp.zeros(gkv_refs[b].shape, BF16)

    gqt_ref[...] = (acc_ref[...] * SCALE).astype(BF16)


def attention_stats(info, qseg, query, window):
    reach = len(window) - 1
    rows = query.shape[0]
    vmem = pl.BlockSpec(memory_space=pltpu.VMEM)
    return pl.pallas_call(
        lambda *refs: stats_kernel(reach, *refs),
        name="attention_stats",
        out_shape=(
            jax.ShapeDtypeStruct((2, rows), F32),
            jax.ShapeDtypeStruct((2 * HD, rows), F32),
        ),
        in_specs=[pl.BlockSpec(memory_space=pltpu.SMEM)] + [vmem] * (reach + 3),
        out_specs=(vmem, vmem),
        scratch_shapes=[
            pltpu.VMEM((2 * HD, rows), BF16),
            pltpu.VMEM((2, rows), F32),
            pltpu.VMEM((2, rows), F32),
        ],
    )(info, qseg, query, *window)


def attention_grads(info, qseg, query, doutt, lse, out, window):
    reach = len(window) - 1
    rows = query.shape[0]
    vmem = pl.BlockSpec(memory_space=pltpu.VMEM)
    result = pl.pallas_call(
        lambda *refs: grads_kernel(reach, *refs),
        name="attention_grads",
        out_shape=(jax.ShapeDtypeStruct((2 * HD, rows), BF16),)
        + (jax.ShapeDtypeStruct((rows, 2 * HD), BF16),) * (reach + 1),
        in_specs=[pl.BlockSpec(memory_space=pltpu.SMEM)] + [vmem] * (reach + 6),
        out_specs=(vmem,) * (reach + 2),
        scratch_shapes=[
            pltpu.VMEM((2 * HD, rows), BF16),
            pltpu.VMEM((rows, 2 * HD), BF16),
            pltpu.VMEM((2, rows), F32),
            pltpu.VMEM((2 * HD, rows), F32),
        ],
    )(info, qseg, query, doutt, lse, out, *window)
    return result[0], result[1:]


def sent_to_all(x, axis):
    copies = jnp.broadcast_to(x, (lax.axis_size(axis), *x.shape))
    return lax.all_to_all(copies, axis, split_axis=0, concat_axis=0, tiled=True)


def local(query, keys, values, grad_out, segment_ids, w_query, w_key, w_value, w_out):
    count = lax.axis_size("aa")
    own = lax.axis_index("aa")
    rows = query.shape[0]
    reach = min(count - 1, -(-(DOC_MOST - 1) // rows))
    all_seg = sent_to_all(segment_ids, "aa").reshape(-1)
    block = jnp.concatenate((keys, values), axis=1)
    window = [
        lax.ppermute(block, "aa", [(i, i + d) for i in range(count - d)])
        for d in range(reach, 0, -1)
    ] + [block]
    gathered = grad_out.T
    for axis in reversed(BA):
        gathered = lax.all_gather(gathered, axis, axis=0, tiled=True)
    starts = jnp.sum(
        (all_seg[None, :] < jnp.arange(DOCS, dtype=jnp.int32)[:, None]).astype(jnp.int32), axis=1
    )
    first_start = jnp.sum((all_seg < segment_ids[0]).astype(jnp.int32))
    lowest = first_start // rows - own + reach
    info = jnp.concatenate((jnp.stack((lowest, own * rows)), starts))
    qseg = segment_ids[None, :]
    lse, out = attention_stats(info, qseg, query, window)
    doutt = dot(w_out, gathered).astype(BF16)
    gqt, partial = attention_grads(info, qseg, query, doutt, lse, out, window)
    total = partial[reach].astype(F32)
    for d in range(1, reach + 1):
        total = total + lax.ppermute(
            partial[reach - d], "aa", [(i + d, i) for i in range(count - d)]
        ).astype(F32)
    gkvt = total.astype(BF16).T
    result = (
        dot(w_query, gqt) + dot(w_key, gkvt[:HD]) + dot(w_value, gkvt[HD:])
    ).astype(BF16)
    for axis in BA:
        result = lax.psum_scatter(result, axis, scatter_dimension=0, tiled=True)
    return result.T


def solution(mesh):
    finer = Mesh(mesh.devices.reshape(mesh.shape["aa"], 8, 2), ("aa", "ba_0", "ba_1"))
    return jax.shard_map(
        local,
        mesh=finer,
        in_specs=(
            P("aa", BA),
            P("aa", BA),
            P("aa", BA),
            P("aa", BA),
            P("aa"),
            P(None, BA),
            P(None, BA),
            P(None, BA),
            P(BA, None),
        ),
        out_specs=P("aa", BA),
        check_vma=False,
    )
```

time: 459 us -> 235 us (0.51)
  matrix products: 88.6 us -> 13.6 us
  waiting for transfers between devices: 177 us -> 114 us
  other arithmetic: 66.9 us -> 4.72 us
  local copies, waits for them, and re-layouts: 53.7 us -> 12.8 us
  Pallas kernels: 0 us -> 11.5 us
  starting transfers between devices: 41.9 us -> 49.9 us
    unnamed x4 -> x5, waiting for transfers between devices: 0.07 us -> 84 us
    reduce_scatter x2 -> x0, waiting for transfers between devices: 75 us -> none  [summed_rows(): x = lax.psum_scatter(x, axis, scatter_dimension=dim, tiled=True)]
    dot_general x86 -> x4, matrix products: 88.6 us -> 13.6 us  [dot(): lax.dot_general(a, b, (((1,), (0,)), ((), ())), preferred_element_type=F32)]
    all_gather x2 -> x1, waiting for transfers between devices: 53.2 us -> 1.14 us  [local(): gathered = lax.all_gather(gathered, axis, axis=0, tiled=True)]
    convert_element_type x32 -> x0, other arithmetic: 50.7 us -> none  [the longest x16 25.4 us: step_keys(): from_behind((dv_now + add_v).astype(jnp.bfloat16), 'aa', 1)]
    while x128 -> x0, local copies, waits for them, and re-layouts: 28.8 us -> none
    ppermute x64 -> x18, waiting for transfers between devices: 46.8 us -> 29.2 us  [the longest x9 21.2 us: local(): lax.ppermute(partial[reach - d], 'aa', [(i + d, i) for i in range(count -...]
    dynamic_slice x17 -> x0, local copies, waits for them, and re-layouts: 13.4 us -> none  [the longest x16 13.3 us: step_keys(): key_seg = lax.dynamic_slice_in_dim(all_seg, anchor * tok_count, tok_count)]
  transfers between devices with their start and end apart: 69 -> 22, of which waited for: 21 -> 14; matrix products, arithmetic and copies ran while one was open for 36% -> 4% of each run, Pallas kernels for 0% -> 2%
where the time goes in v1:
time: 235 us; the launch traced here: 234 us
  waiting for transfers between devices  114 us (49%)
  starting transfers between devices  49.9 us (21%)
  between operations  15.4 us (7%)
  matrix products  13.6 us (6%)
  local copies, waits for them, and re-layouts  12.8 us (5%)
  blocking collectives  12.1 us (5%)
  Pallas kernels  11.5 us (5%)
  other arithmetic  4.72 us (2%)
    unnamed x5, waiting for transfers between devices  84 us
    ppermute x9, starting transfers between devices, local(): lax.ppermute(block, 'aa', [(i, i + d) for i in range(count - d)])  22 us
    ppermute x9, waiting for transfers between devices, local(): lax.ppermute(partial[reach - d], 'aa', [(i + d, i) for i in range(count -...  21.2 us
    ppermute x9, starting transfers between devices, local(): lax.ppermute(partial[reach - d], 'aa', [(i + d, i) for i in range(count -...  21.1 us
    dot_general x4, matrix products, dot(): lax.dot_general(a, b, (((1,), (0,)), ((), ())), preferred_element_type=F32)  13.6 us
    all_gather x1, blocking collectives, local(): gathered = lax.all_gather(gathered, axis, axis=0, tiled=True)  12.1 us
    unnamed x20, local copies, waits for them, and re-layouts  8.09 us
    ppermute x9, waiting for transfers between devices, local(): lax.ppermute(block, 'aa', [(i, i + d) for i in range(count - d)])  8.02 us
  transfers between devices with their start and end apart: 22, of which 14 were waited for; matrix products, arithmetic and copies ran while one was open for 4% of the time, Pallas kernels for 2%

profile of v1, /device:TPU:24, one launch (start us, length us, event | category | flops | bytes accessed | tf_op | source)
XLA Modules:
  0.0 234.4 jit_solution(11015890902850724309)
XLA Ops:
  6.5 12.1 %all_gather.6 = bf16[672,384]{1,0:T(8,128)(2,1)} all-gather(bf16[336,384]{1,0:T(8,128)(2,1)} %bitcast.19), channel_id=1, replica_groups=mesh['aa'=16,'ba_0'=8,'ba_1'=2] {'ba_1'}, dimensions={0}, use_global_device_ids=true | all-gather | bytes 774144 | tf_op jit(solution)/shard_map/all_gather | solution.py:181
  18.6 0.0 all-gather.2.cloned.1.call-update
  18.6 0.9 constant_dynamic-update-slice_fusion.1
  19.5 0.9 constant_dynamic-update-slice_fusion.refs_12_.refs_15_
  20.5 1.9 collective-permute-start.8
  22.4 2.2 collective-permute-start.7
  24.6 4.5 %collective-permute-start.6 = (bf16[384,256]{1,0:T(8,128)(2,1)S(1)}, bf16[384,256]{1,0:T(8,128)(2,1)S(1)}, u32[]{:S(2)}, u32[]{:S(2)}) collective-permute-start(bf16[384,256]{1,0:T(8,128)(2,1)S(1)} %constant_dynamic-update-slice_fusion.refs_12_.refs_15_), channel_id=1, source_target_pairs={{0,48},{16,64},{32,80},{48,96},{64,112},{80,128},{96,144},{112,160... | collective-permute-start | bytes 589832 | tf_op jit(solution)/shard_map/ppermute | solution.py:176
  29.1 2.9 %collective-permute-start.5 = (bf16[384,256]{1,0:T(8,128)(2,1)S(1)}, bf16[384,256]{1,0:T(8,128)(2,1)}, u32[]{:S(2)}, u32[]{:S(2)}) collective-permute-start(bf16[384,256]{1,0:T(8,128)(2,1)S(1)} %constant_dynamic-update-slice_fusion.refs_12_.refs_15_), channel_id=1, source_target_pairs={{0,64},{16,80},{32,96},{48,112},{64,128},{80,144},{96,160},{112,17... | collective-permute-start | bytes 589832 | tf_op jit(solution)/shard_map/ppermute | solution.py:176
  32.0 1.3 broadcast_in_dim.7
  33.3 6.7 %all-to-all-start = ((s32[16,1,384]{2,1,0:T(1,128)}), s32[16,1,384]{2,1,0:T(1,128)}, u32[]{:S(2)}, u32[]{:S(2)}) async-start(s32[16,1,384]{2,1,0:T(1,128)} %broadcast_in_dim.7), calls=%async_computation | async-start | bytes 49152 | tf_op jit(solution)/shard_map/all_to_all | solution.py:165
  40.0 0.0 reduce-scatter.7.cloned.1.call-start
  40.0 4.0 %collective-permute-start.4 = (bf16[384,256]{1,0:T(8,128)(2,1)S(1)}, bf16[384,256]{1,0:T(8,128)(2,1)}, u32[]{:S(2)}, u32[]{:S(2)}) collective-permute-start(bf16[384,256]{1,0:T(8,128)(2,1)S(1)} %constant_dynamic-update-slice_fusion.refs_12_.refs_15_), channel_id=1, source_target_pairs={{0,80},{16,96},{32,112},{48,128},{64,144},{80,160},{96,176},{112,1... | collective-permute-start | bytes 589832 | tf_op jit(solution)/shard_map/ppermute | solution.py:176
  44.1 1.2 slice.9
  45.3 1.3 broadcast_in_dim.8.refs_1_
  46.6 0.0 all-to-all-done
  46.6 2.0 convert_reduce_fusion.1
  50.6 0.0 collective-permute-done.8.refs_11_.refs_14_
  50.6 1.9 collective-permute-start.3
  52.5 0.0 collective-permute-done.7.refs_10_.refs_13_
  52.5 1.3 collective-permute-start.2
  53.8 0.0 collective-permute-done.6.refs_9_.refs_12_
  53.9 1.3 collective-permute-start.1
  55.2 0.0 collective-permute-done.5.refs_8_.refs_11_
  55.2 2.0 collective-permute-start
  57.2 0.9 convert_reduce_fusion
  58.1 0.6 pad_add_fusion.refs_0_
  58.7 0.0 collective-permute-done.4.refs_7_.refs_10_
  58.7 1.6 collective-permute-done.3.refs_6_.refs_9_
  60.3 1.7 collective-permute-done.2.refs_5_.refs_8_
  62.0 3.3 %collective-permute-done.1.refs_4_.refs_7_ = bf16[384,256]{1,0:T(8,128)(2,1)S(1)} collective-permute-done((bf16[384,256]{1,0:T(8,128)(2,1)S(1)}, bf16[384,256]{1,0:T(8,128)(2,1)S(1)}, u32[]{:S(2)}, u32[]{:S(2)}) %collective-permute-start.1) | collective-permute-done | bytes 196640 | tf_op jit(solution)/shard_map/ppermute | solution.py:176
  65.3 0.7 copy-done.8
  66.0 1.4 collective-permute-done.refs_3_.refs_6_
  67.4 5.5 %attention_stats.1 = (f32[2,384]{1,0:T(2,128)}, f32[256,384]{1,0:T(8,128)}) custom-call(s32[8]{0:T(128)} %pad_add_fusion.refs_0_, s32[1,384]{1,0:T(1,128)} %broadcast_in_dim.8.refs_1_, bf16[384,256]{1,0:T(8,128)(2,1)} %refs_2_.3, bf16[384,256]{1,0:T(8,128)(2,1)} %collective-permute-done.refs_3_.refs_6_, bf16[384,256]{1,0:T(8,128)(2,1)} %copy-done.8, ...), custom_call_target="tpu_custom_call" | custom-call | tf_op jit(solution)/shard_map/attention_stats/pallas_call | solution.py:125
  73.0 1.1 all-gather.2.cloned.1.call-done
  74.1 5.3 %convolution_convert_fusion.refs_3_ = bf16[256,384]{1,0:T(8,128)(2,1)} fusion(bf16[256,5376]{1,0:T(8,128)(2,1)} %param.17, bf16[5376,384]{1,0:T(8,128)(2,1)} %all-gather.2.cloned.1.call-done), kind=kOutput, calls=%fused_computation.4 | convolution fusion | flops 1057062912 | bytes 7077888 | tf_op jit(solution)/shard_map/dot_general | solution.py:25
  79.4 6.0 %attention_grads.1 = (bf16[256,384]{1,0:T(8,128)(2,1)}, bf16[384,256]{1,0:T(8,128)(2,1)}, bf16[384,256]{1,0:T(8,128)(2,1)}, bf16[384,256]{1,0:T(8,128)(2,1)}, bf...) custom-call(s32[8]{0:T(128)} %pad_add_fusion.refs_0_, ...), custom_call_target="tpu_custom_call" | custom-call | tf_op jit(solution)/shard_map/attention_grads/pallas_call | solution.py:146
  85.4 3.1 %collective-permute-start.9 = (bf16[384,256]{1,0:T(8,128)(2,1)}, bf16[384,256]{1,0:T(8,128)(2,1)S(1)}, u32[]{:S(2)}, u32[]{:S(2)}) collective-permute-start(bf16[384,256]{1,0:T(8,128)(2,1)} %get-tuple-element.22), channel_id=1, source_target_pairs={{16,0},{32,16},{48,32},{64,48},{80,64},{96,80},{112,96},{128,112},... | collective-permute-start | bytes 589832 | tf_op jit(solution)/shard_map/ppermute | solution.py:194
  88.5 6.5 %collective-permute-start.10 = (bf16[384,256]{1,0:T(8,128)(2,1)}, bf16[384,256]{1,0:T(8,128)(2,1)S(1)}, u32[]{:S(2)}, u32[]{:S(2)}) collective-permute-start(bf16[384,256]{1,0:T(8,128)(2,1)} %get-tuple-element.23), channel_id=1, source_target_pairs={{32,0},{48,16},{64,32},{80,48},{96,64},{112,80},{128,96},{144,112}... | collective-permute-start | bytes 589832 | tf_op jit(solution)/shard_map/ppermute | solution.py:194
  95.0 2.0 collective-permute-start.11
  97.0 1.9 collective-permute-start.12
  98.9 1.9 collective-permute-start.13
  100.8 0.0 collective-permute-done.9
  100.8 1.9 collective-permute-start.14
  102.8 1.3 collective-permute-start.15
  104.1 2.3 collective-permute-done.11
  106.4 1.3 collective-permute-start.16
  107.7 3.0 %collective-permute-done.12 = bf16[384,256]{1,0:T(8,128)(2,1)S(1)} collective-permute-done((bf16[384,256]{1,0:T(8,128)(2,1)}, bf16[384,256]{1,0:T(8,128)(2,1)S(1)}, u32[]{:S(2)}, u32[]{:S(2)}) %collective-permute-start.12) | collective-permute-done | bytes 196640 | tf_op jit(solution)/shard_map/ppermute | solution.py:194
  110.7 1.3 collective-permute-start.17
  112.0 7.7 %collective-permute-done.13 = bf16[384,256]{1,0:T(8,128)(2,1)S(1)} collective-permute-done((bf16[384,256]{1,0:T(8,128)(2,1)}, bf16[384,256]{1,0:T(8,128)(2,1)S(1)}, u32[]{:S(2)}, u32[]{:S(2)}) %collective-permute-start.13) | collective-permute-done | bytes 196640 | tf_op jit(solution)/shard_map/ppermute | solution.py:194
  119.6 3.5 %collective-permute-done.14 = bf16[384,256]{1,0:T(8,128)(2,1)S(1)} collective-permute-done((bf16[384,256]{1,0:T(8,128)(2,1)}, bf16[384,256]{1,0:T(8,128)(2,1)S(1)}, u32[]{:S(2)}, u32[]{:S(2)}) %collective-permute-start.14) | collective-permute-done | bytes 196640 | tf_op jit(solution)/shard_map/ppermute | solution.py:194
  123.2 1.0 collective-permute-done.15
  124.2 1.3 collective-permute-done.16
  125.5 2.3 %collective-permute-done.17 = bf16[384,256]{1,0:T(8,128)(2,1)S(1)} collective-permute-done((bf16[384,256]{1,0:T(8,128)(2,1)}, bf16[384,256]{1,0:T(8,128)(2,1)S(1)}, u32[]{:S(2)}, u32[]{:S(2)}) %collective-permute-start.17) | collective-permute-done | bytes 196640 | tf_op jit(solution)/shard_map/ppermute | solution.py:194
  127.9 1.2 fusion.3
  129.0 0.0 copy-start.1
  129.1 2.7 %fusion.4 = f32[384,5376]{1,0:T(8,128)S(1)} fusion(bf16[5376,128]{1,0:T(8,128)(2,1)} %param.16, bf16[256,384]{0,1:T(8,128)(2,1)S(1)} %fusion.3), kind=kOutput, calls=%fused_computation.9 | convolution fusion | flops 528482304 | bytes 9732096 | tf_op jit(solution)/shard_map/dot_general | solution.py:25
  131.8 1.2 fusion.6
  133.0 4.4 %fusion.2 = bf16[5376,384]{0,1:T(8,128)(2,1)} fusion(f32[384,5376]{1,0:T(8,128)S(1)} %fusion.4, f32[384,5376]{1,0:T(8,128)S(1)} %fusion.6, bf16[256,384]{1,0:T(8,128)(2,1)} %get-tuple-element.20, bf16[5376,256]{1,0:T(8,128)(2,1)S(1)} %copy-done), kind=kOutput, calls=%fused_computation.3 | convolution fusion | flops 1063157760 | bytes 23592960 | tf_op jit(solution)/shard_map/dot_general | solution.py:25
  137.4 6.4 %copy.17 = bf16[5376,384]{1,0:T(8,128)(2,1)} copy(bf16[5376,384]{0,1:T(8,128)(2,1)} %fusion.2) | data formatting | bytes 8257536
  143.9 0.0 reduce-scatter.7.cloned.1.call-update
  143.9 0.0 reduce-scatter.9.cloned.1.call-start
  144.0 61.6 %reduce-scatter.7.cloned.1.call-done = bf16[672,384]{1,0:T(8,128)(2,1)} async-done(((bf16[5376,384]{1,0:T(8,128)(2,1)}), bf16[672,384]{1,0:T(8,128)(2,1)}) %reduce-scatter.7.cloned.1.call-update) | async-done | bytes 516112
  205.6 0.0 reduce-scatter.9.cloned.1.call-update
  205.6 22.3 %reduce-scatter.9.cloned.1.call-done = bf16[336,384]{1,0:T(8,128)(2,1)} async-done(((bf16[672,384]{1,0:T(8,128)(2,1)}), bf16[336,384]{1,0:T(8,128)(2,1)}) %reduce-scatter.9.cloned.1.call-update) | async-done | bytes 258064
  (18 shorter events, 0.0 us)
Async XLA Ops:
  6.5 126.5 %copy-start = (bf16[5376,256]{1,0:T(8,128)(2,1)S(1)}, bf16[5376,256]{1,0:T(8,128)(2,1)}, u32[]{:S(2)}) copy-start(bf16[5376,256]{1,0:T(8,128)(2,1)} %param.14) | copy-start | bytes 8257540
  6.5 67.6 %all-gather.2.cloned.1.call-start = ((), (), s32[]{:S(2)}) async-start(), calls=%async_computation.3 | async-start | bytes 4644864 | tf_op jit(solution)/shard_map/all_gather | solution.py:181
  20.5 47.0 %copy-start.2 = (bf16[384,256]{1,0:T(8,128)(2,1)}, bf16[384,256]{1,0:T(8,128)(2,1)S(1)}, u32[]{:S(2)}) copy-start(bf16[384,256]{1,0:T(8,128)(2,1)S(1)} %constant_dynamic-update-slice_fusion.refs_12_.refs_15_) | copy-start | bytes 589828
  20.5 30.1 %collective-permute-start.8 = (bf16[384,256]{1,0:T(8,128)(2,1)S(1)}, bf16[384,256]{1,0:T(8,128)(2,1)S(1)}, u32[]{:S(2)}, u32[]{:S(2)}) collective-permute-start(bf16[384,256]{1,0:T(8,128)(2,1)S(1)} %constant_dynamic-update-slice_fusion.refs_12_.refs_15_), channel_id=1, source_target_pairs={{0,16},{16,32},{32,48},{48,64},{64,80},{80,96},{96,112},{112,128},... | collective-permute-start | bytes 589832 | tf_op jit(solution)/shard_map/ppermute | solution.py:176
  22.4 30.1 %collective-permute-start.7 = (bf16[384,256]{1,0:T(8,128)(2,1)S(1)}, bf16[384,256]{1,0:T(8,128)(2,1)S(1)}, u32[]{:S(2)}, u32[]{:S(2)}) collective-permute-start(bf16[384,256]{1,0:T(8,128)(2,1)S(1)} %constant_dynamic-update-slice_fusion.refs_12_.refs_15_), channel_id=1, source_target_pairs={{0,32},{16,48},{32,64},{48,80},{64,96},{80,112},{96,128},{112,144}... | collective-permute-start | bytes 589832 | tf_op jit(solution)/shard_map/ppermute | solution.py:176
  24.6 29.3 %collective-permute-start.6 = (bf16[384,256]{1,0:T(8,128)(2,1)S(1)}, bf16[384,256]{1,0:T(8,128)(2,1)S(1)}, u32[]{:S(2)}, u32[]{:S(2)}) collective-permute-start(bf16[384,256]{1,0:T(8,128)(2,1)S(1)} %constant_dynamic-update-slice_fusion.refs_12_.refs_15_), channel_id=1, source_target_pairs={{0,48},{16,64},{32,80},{48,96},{64,112},{80,128},{96,144},{112,160... | collective-permute-start | bytes 589832 | tf_op jit(solution)/shard_map/ppermute | solution.py:176
  29.1 26.1 %collective-permute-start.5 = (bf16[384,256]{1,0:T(8,128)(2,1)S(1)}, bf16[384,256]{1,0:T(8,128)(2,1)}, u32[]{:S(2)}, u32[]{:S(2)}) collective-permute-start(bf16[384,256]{1,0:T(8,128)(2,1)S(1)} %constant_dynamic-update-slice_fusion.refs_12_.refs_15_), channel_id=1, source_target_pairs={{0,64},{16,80},{32,96},{48,112},{64,128},{80,144},{96,160},{112,17... | collective-permute-start | bytes 589832 | tf_op jit(solution)/shard_map/ppermute | solution.py:176
  33.3 13.3 %all-to-all-start = ((s32[16,1,384]{2,1,0:T(1,128)}), s32[16,1,384]{2,1,0:T(1,128)}, u32[]{:S(2)}, u32[]{:S(2)}) async-start(s32[16,1,384]{2,1,0:T(1,128)} %broadcast_in_dim.7), calls=%async_computation | async-start | bytes 49152 | tf_op jit(solution)/shard_map/all_to_all | solution.py:165
  40.0 165.6 %reduce-scatter.7.cloned.1.call-start = ((), (), s32[]{:S(2)}) async-start(), calls=%async_computation.4 | async-start | bytes 4644864
  40.0 18.7 %collective-permute-start.4 = (bf16[384,256]{1,0:T(8,128)(2,1)S(1)}, bf16[384,256]{1,0:T(8,128)(2,1)}, u32[]{:S(2)}, u32[]{:S(2)}) collective-permute-start(bf16[384,256]{1,0:T(8,128)(2,1)S(1)} %constant_dynamic-update-slice_fusion.refs_12_.refs_15_), channel_id=1, source_target_pairs={{0,80},{16,96},{32,112},{48,128},{64,144},{80,160},{96,176},{112,1... | collective-permute-start | bytes 589832 | tf_op jit(solution)/shard_map/ppermute | solution.py:176
  50.6 16.9 %copy-start.3 = (bf16[384,256]{1,0:T(8,128)(2,1)}, bf16[384,256]{1,0:T(8,128)(2,1)S(1)}, u32[]{:S(2)}) copy-start(bf16[384,256]{1,0:T(8,128)(2,1)S(1)} %collective-permute-done.8.refs_11_.refs_14_) | copy-start | bytes 589828
  50.6 9.7 %collective-permute-start.3 = (bf16[384,256]{1,0:T(8,128)(2,1)S(1)}, bf16[384,256]{1,0:T(8,128)(2,1)S(1)}, u32[]{:S(2)}, u32[]{:S(2)}) collective-permute-start(bf16[384,256]{1,0:T(8,128)(2,1)S(1)} %constant_dynamic-update-slice_fusion.refs_12_.refs_15_), channel_id=1, source_target_pairs={{0,96},{16,112},{32,128},{48,144},{64,160},{80,176},{96,192},{112,... | collective-permute-start | bytes 589832 | tf_op jit(solution)/shard_map/ppermute | solution.py:176
  52.5 14.9 %copy-start.4 = (bf16[384,256]{1,0:T(8,128)(2,1)}, bf16[384,256]{1,0:T(8,128)(2,1)S(1)}, u32[]{:S(2)}) copy-start(bf16[384,256]{1,0:T(8,128)(2,1)S(1)} %collective-permute-done.7.refs_10_.refs_13_) | copy-start | bytes 589828
  52.5 9.5 %collective-permute-start.2 = (bf16[384,256]{1,0:T(8,128)(2,1)S(1)}, bf16[384,256]{1,0:T(8,128)(2,1)S(1)}, u32[]{:S(2)}, u32[]{:S(2)}) collective-permute-start(bf16[384,256]{1,0:T(8,128)(2,1)S(1)} %constant_dynamic-update-slice_fusion.refs_12_.refs_15_), channel_id=1, source_target_pairs={{0,112},{16,128},{32,144},{48,160},{64,176},{80,192},{96,208},{112... | collective-permute-start | bytes 589832 | tf_op jit(solution)/shard_map/ppermute | solution.py:176
  53.8 13.6 %copy-start.5 = (bf16[384,256]{1,0:T(8,128)(2,1)}, bf16[384,256]{1,0:T(8,128)(2,1)S(1)}, u32[]{:S(2)}) copy-start(bf16[384,256]{1,0:T(8,128)(2,1)S(1)} %collective-permute-done.6.refs_9_.refs_12_) | copy-start | bytes 589828
  53.9 11.5 %collective-permute-start.1 = (bf16[384,256]{1,0:T(8,128)(2,1)S(1)}, bf16[384,256]{1,0:T(8,128)(2,1)S(1)}, u32[]{:S(2)}, u32[]{:S(2)}) collective-permute-start(bf16[384,256]{1,0:T(8,128)(2,1)S(1)} %constant_dynamic-update-slice_fusion.refs_12_.refs_15_), channel_id=1, source_target_pairs={{0,128},{16,144},{32,160},{48,176},{64,192},{80,208},{96,224},{112... | collective-permute-start | bytes 589832 | tf_op jit(solution)/shard_map/ppermute | solution.py:176
  55.2 12.2 %collective-permute-start = (bf16[384,256]{1,0:T(8,128)(2,1)S(1)}, bf16[384,256]{1,0:T(8,128)(2,1)}, u32[]{:S(2)}, u32[]{:S(2)}) collective-permute-start(bf16[384,256]{1,0:T(8,128)(2,1)S(1)} %constant_dynamic-update-slice_fusion.refs_12_.refs_15_), channel_id=1, source_target_pairs={{0,144},{16,160},{32,176},{48,192},{64,208},{80,224},{96,240},{1,1... | collective-permute-start | bytes 589832 | tf_op jit(solution)/shard_map/ppermute | solution.py:176
  60.3 5.0 %copy-start.6 = (bf16[384,256]{1,0:T(8,128)(2,1)}, bf16[384,256]{1,0:T(8,128)(2,1)S(1)}, u32[]{:S(2)}) copy-start(bf16[384,256]{1,0:T(8,128)(2,1)S(1)} %collective-permute-done.3.refs_6_.refs_9_) | copy-start | bytes 589828
  62.0 3.3 %copy-start.7 = (bf16[384,256]{1,0:T(8,128)(2,1)}, bf16[384,256]{1,0:T(8,128)(2,1)S(1)}, u32[]{:S(2)}) copy-start(bf16[384,256]{1,0:T(8,128)(2,1)S(1)} %collective-permute-done.2.refs_5_.refs_8_) | copy-start | bytes 589828
  65.3 0.7 copy-start.8
  85.4 15.4 %collective-permute-start.9 = (bf16[384,256]{1,0:T(8,128)(2,1)}, bf16[384,256]{1,0:T(8,128)(2,1)S(1)}, u32[]{:S(2)}, u32[]{:S(2)}) collective-permute-start(bf16[384,256]{1,0:T(8,128)(2,1)} %get-tuple-element.22), channel_id=1, source_target_pairs={{16,0},{32,16},{48,32},{64,48},{80,64},{96,80},{112,96},{128,112},... | collective-permute-start | bytes 589832 | tf_op jit(solution)/shard_map/ppermute | solution.py:194
  88.5 14.2 %collective-permute-start.10 = (bf16[384,256]{1,0:T(8,128)(2,1)}, bf16[384,256]{1,0:T(8,128)(2,1)S(1)}, u32[]{:S(2)}, u32[]{:S(2)}) collective-permute-start(bf16[384,256]{1,0:T(8,128)(2,1)} %get-tuple-element.23), channel_id=1, source_target_pairs={{32,0},{48,16},{64,32},{80,48},{96,64},{112,80},{128,96},{144,112}... | collective-permute-start | bytes 589832 | tf_op jit(solution)/shard_map/ppermute | solution.py:194
  95.0 11.4 %collective-permute-start.11 = (bf16[384,256]{1,0:T(8,128)(2,1)}, bf16[384,256]{1,0:T(8,128)(2,1)S(1)}, u32[]{:S(2)}, u32[]{:S(2)}) collective-permute-start(bf16[384,256]{1,0:T(8,128)(2,1)} %get-tuple-element.24), channel_id=1, source_target_pairs={{48,0},{64,16},{80,32},{96,48},{112,64},{128,80},{144,96},{160,112... | collective-permute-start | bytes 589832 | tf_op jit(solution)/shard_map/ppermute | solution.py:194
  97.0 13.7 %collective-permute-start.12 = (bf16[384,256]{1,0:T(8,128)(2,1)}, bf16[384,256]{1,0:T(8,128)(2,1)S(1)}, u32[]{:S(2)}, u32[]{:S(2)}) collective-permute-start(bf16[384,256]{1,0:T(8,128)(2,1)} %get-tuple-element.25), channel_id=1, source_target_pairs={{64,0},{80,16},{96,32},{112,48},{128,64},{144,80},{160,96},{176,11... | collective-permute-start | bytes 589832 | tf_op jit(solution)/shard_map/ppermute | solution.py:194
  98.9 20.7 %collective-permute-start.13 = (bf16[384,256]{1,0:T(8,128)(2,1)}, bf16[384,256]{1,0:T(8,128)(2,1)S(1)}, u32[]{:S(2)}, u32[]{:S(2)}) collective-permute-start(bf16[384,256]{1,0:T(8,128)(2,1)} %get-tuple-element.26), channel_id=1, source_target_pairs={{80,0},{96,16},{112,32},{128,48},{144,64},{160,80},{176,96},{192,1... | collective-permute-start | bytes 589832 | tf_op jit(solution)/shard_map/ppermute | solution.py:194
  100.8 22.3 %collective-permute-start.14 = (bf16[384,256]{1,0:T(8,128)(2,1)}, bf16[384,256]{1,0:T(8,128)(2,1)S(1)}, u32[]{:S(2)}, u32[]{:S(2)}) collective-permute-start(bf16[384,256]{1,0:T(8,128)(2,1)} %get-tuple-element.27), channel_id=1, source_target_pairs={{96,0},{112,16},{128,32},{144,48},{160,64},{176,80},{192,96},{208,... | collective-permute-start | bytes 589832 | tf_op jit(solution)/shard_map/ppermute | solution.py:194
  102.8 21.4 %collective-permute-start.15 = (bf16[384,256]{1,0:T(8,128)(2,1)}, bf16[384,256]{1,0:T(8,128)(2,1)S(1)}, u32[]{:S(2)}, u32[]{:S(2)}) collective-permute-start(bf16[384,256]{1,0:T(8,128)(2,1)} %get-tuple-element.28), channel_id=1, source_target_pairs={{112,0},{128,16},{144,32},{160,48},{176,64},{192,80},{208,96},{224... | collective-permute-start | bytes 589832 | tf_op jit(solution)/shard_map/ppermute | solution.py:194
  106.4 19.1 %collective-permute-start.16 = (bf16[384,256]{1,0:T(8,128)(2,1)}, bf16[384,256]{1,0:T(8,128)(2,1)S(1)}, u32[]{:S(2)}, u32[]{:S(2)}) collective-permute-start(bf16[384,256]{1,0:T(8,128)(2,1)} %get-tuple-element.29), channel_id=1, source_target_pairs={{128,0},{144,16},{160,32},{176,48},{192,64},{208,80},{224,96},{240... | collective-permute-start | bytes 589832 | tf_op jit(solution)/shard_map/ppermute | solution.py:194
  110.7 17.2 %collective-permute-start.17 = (bf16[384,256]{1,0:T(8,128)(2,1)}, bf16[384,256]{1,0:T(8,128)(2,1)S(1)}, u32[]{:S(2)}, u32[]{:S(2)}) collective-permute-start(bf16[384,256]{1,0:T(8,128)(2,1)} %get-tuple-element.30), channel_id=1, source_target_pairs={{144,0},{160,16},{176,32},{192,48},{208,64},{224,80},{240,96},{145... | collective-permute-start | bytes 589832 | tf_op jit(solution)/shard_map/ppermute | solution.py:194
  129.0 2.7 %copy-start.1 = (bf16[5376,128]{1,0:T(8,128)(2,1)S(1)}, bf16[5376,128]{1,0:T(8,128)(2,1)}, u32[]{:S(2)}) copy-start(bf16[5376,128]{1,0:T(8,128)(2,1)} %param.15) | copy-start | bytes 4128772
  143.9 84.0 %reduce-scatter.9.cloned.1.call-start = ((), (), s32[]{:S(2)}) async-start(), calls=%async_computation.5 | async-start | bytes 774144
Sparse Core Ops, SparseCore 0:
  18.7 55.3 all-gather.1
  144.0 61.4 reduce-scatter.6
  208.1 19.7 reduce-scatter.8

commit v2 on v1

v2 whole, which is shorter than its diff:
```python
import math

import jax
import jax.numpy as jnp
from jax import lax
from jax.experimental import pallas as pl
from jax.experimental.pallas import tpu as pltpu
from jax.sharding import Mesh
from jax.sharding import PartitionSpec as P

D = 5376
HQ = 32
HD = 128
DOCS = 6
DOC_MOST = 3456
ROWS = 384
HALF = 5
BLOCKS = 2 * HALF
SEG_ROWS = 16
PACKED = ROWS + SEG_ROWS
FEATS = 336
RING = 8
AA = ("xl", "y", "core")
BA = ("z", "xh")
NEG_FILL = -1e30
SCALE = (D / HQ) ** (-0.5)
SCALE2 = SCALE * math.log2(math.e)
F32 = jnp.float32
BF16 = jnp.bfloat16
VMEM = pl.BlockSpec(memory_space=pltpu.VMEM)
SMEM = pl.BlockSpec(memory_space=pltpu.SMEM)
ANY = pl.BlockSpec(memory_space=pl.ANY)


def dot(a, b):
    return lax.dot_general(a, b, (((1,), (0,)), ((), ())), preferred_element_type=F32)


def load_window(kv_refs, buf, sem):
    copies = [pltpu.make_async_copy(kv_refs[b], buf.at[b], sem.at[b]) for b in range(BLOCKS)]
    for c in copies:
        c.start()
    return copies


def stats_kernel(own_ref, qseg_ref, q_ref, *refs):
    kv_refs = refs[:BLOCKS]
    lse_ref, out_ref, start_ref, low_ref, buf, qt_ref, m_ref, l_ref, sem = refs[BLOCKS:]
    copies = load_window(kv_refs, buf, sem)
    own = own_ref[0]
    qt_ref[...] = q_ref[...].T
    m_ref[...] = jnp.full(m_ref.shape, NEG_FILL, F32)
    l_ref[...] = jnp.zeros(l_ref.shape, F32)
    out_ref[...] = jnp.zeros(out_ref.shape, F32)
    seg = qseg_ref[...]
    seg0 = jnp.min(seg, axis=1, keepdims=True)
    for c in copies:
        c.wait()
    count = jnp.zeros((SEG_ROWS, HD), jnp.int32)
    line = lax.broadcasted_iota(jnp.int32, (SEG_ROWS, HD), 0)
    for b in range(BLOCKS - 1):
        ids = buf[b, ROWS:, :HD].astype(F32).astype(jnp.int32)
        before = (line < ROWS // HD) & (ids < seg0) & (own + b >= BLOCKS - 1)
        count = count + before.astype(jnp.int32)
    start0 = jnp.sum(count) + jnp.maximum(own - (BLOCKS - 1), 0) * ROWS
    start = jnp.zeros((1, ROWS), jnp.int32) + start0
    for s in range(1, DOCS):
        here = own * ROWS + jnp.sum((seg < s).astype(jnp.int32), axis=1, keepdims=True)
        start = jnp.where((seg == s) & (seg > seg0), here, start)
    start_ref[...] = start
    lowest = lax.div(start0, ROWS) - own + (BLOCKS - 1)
    low_ref[0] = lowest
    pos = own * ROWS + lax.broadcasted_iota(jnp.int32, (1, ROWS), 1)
    key_at = lax.broadcasted_iota(jnp.int32, (ROWS, ROWS), 0)

    def one_block(b, carry):
        first = (own + b - (BLOCKS - 1)) * ROWS
        allowed = (key_at >= start - first) & (key_at <= pos - first)
        kb = buf[b, :ROWS, :HD]
        vt = buf[b, :ROWS, HD:].T
        for h in range(2):
            part = slice(h * HD, (h + 1) * HD)
            s = jnp.where(allowed, dot(kb, qt_ref[part, :]) * SCALE2, NEG_FILL)
            m_old = m_ref[h : h + 1, :]
            m_new = jnp.maximum(m_old, jnp.max(s, axis=0, keepdims=True))
            p = jnp.exp2(s - m_new)
            back = jnp.exp2(m_old - m_new)
            l_ref[h : h + 1, :] = l_ref[h : h + 1, :] * back + jnp.sum(p, axis=0, keepdims=True)
            m_ref[h : h + 1, :] = m_new
            high = p.astype(BF16)
            low = (p - high.astype(F32)).astype(BF16)
            out_ref[part, :] = out_ref[part, :] * back + (dot(vt, high) + dot(vt, low))
        return carry

    lax.fori_loop(lowest, BLOCKS, one_block, 0)
    lse_ref[...] = m_ref[...] + jnp.log2(l_ref[...])
    for h in range(2):
        part = slice(h * HD, (h + 1) * HD)
        out_ref[part, :] = out_ref[part, :] / l_ref[h : h + 1, :]


def grads_kernel(own_ref, low_ref, start_ref, q_ref, doutt_ref, lse_ref, out_ref, *refs):
    kv_refs = refs[:BLOCKS]
    gqt_ref, mine_ref, theirs_ref, buf, qt_ref, dout_ref, delta_ref, acc_ref, sem = refs[BLOCKS:]
    copies = load_window(kv_refs, buf, sem)
    own = own_ref[0]
    lowest = low_ref[0]
    qt_ref[...] = q_ref[...].T
    dout_ref[...] = doutt_ref[...].T
    for h in range(2):
        part = slice(h * HD, (h + 1) * HD)
        delta_ref[h : h + 1, :] = jnp.sum(
            doutt_ref[part, :].astype(F32) * out_ref[part, :], axis=0, keepdims=True
        )
    acc_ref[...] = jnp.zeros(acc_ref.shape, F32)
    start = start_ref[...]
    pos = own * ROWS + lax.broadcasted_iota(jnp.int32, (1, ROWS), 1)
    key_at = lax.broadcasted_iota(jnp.int32, (ROWS, ROWS), 0)
    for c in copies:
        c.wait()

    def one_block(b, target, d):
        @pl.when(b >= lowest)
        def _():
            first = (own + b - (BLOCKS - 1)) * ROWS
            allowed = (key_at >= start - first) & (key_at <= pos - first)
            kb = buf[b, :ROWS, :HD]
            vb = buf[b, :ROWS, HD:]
            kt = kb.T
            gk = gv = None
            for h in range(2):
                part = slice(h * HD, (h + 1) * HD)
                s = dot(kb, qt_ref[part, :]) * SCALE2
                dp = dot(vb, doutt_ref[part, :])
                p = jnp.where(allowed, jnp.exp2(s - lse_ref[h : h + 1, :]), 0.0)
                ds = (p * (dp - delta_ref[h : h + 1, :])).astype(BF16)
                add_v = dot(p.astype(BF16), dout_ref[:, part])
                add_k = dot(ds, q_ref[:, part])
                gv = add_v if h == 0 else gv + add_v
                gk = add_k if h == 0 else gk + add_k
                acc_ref[part, :] += dot(kt, ds)
            target[d, :, :HD] = (gk * SCALE).astype(BF16)
            target[d, :, HD:] = gv.astype(BF16)

        @pl.when(b < lowest)
        def _():
            target[d] = jnp.zeros((ROWS, 2 * HD), BF16)

    def two_blocks(d, carry):
        one_block(BLOCKS - 1 - 2 * d, mine_ref, d)
        one_block(BLOCKS - 2 - 2 * d, theirs_ref, d)
        return carry

    lax.fori_loop(0, HALF, two_blocks, 0)
    gqt_ref[...] = (acc_ref[...] * SCALE).astype(BF16)


def attention_stats(own, qseg, query, window):
    return pl.pallas_call(
        stats_kernel,
        name="attention_stats",
        out_shape=(
            jax.ShapeDtypeStruct((2, ROWS), F32),
            jax.ShapeDtypeStruct((2 * HD, ROWS), F32),
            jax.ShapeDtypeStruct((1, ROWS), jnp.int32),
            jax.ShapeDtypeStruct((1,), jnp.int32),
        ),
        in_specs=[SMEM, VMEM, VMEM] + [ANY] * BLOCKS,
        out_specs=(VMEM, VMEM, VMEM, SMEM),
        scratch_shapes=[
            pltpu.VMEM((BLOCKS, PACKED, 2 * HD), BF16),
            pltpu.VMEM((2 * HD, ROWS), BF16),
            pltpu.VMEM((2, ROWS), F32),
            pltpu.VMEM((2, ROWS), F32),
            pltpu.SemaphoreType.DMA((BLOCKS,)),
        ],
    )(own, qseg, query, *window)


def attention_grads(own, stats, query, doutt, window):
    lse, out, start, lowest = stats
    return pl.pallas_call(
        grads_kernel,
        name="attention_grads",
        out_shape=(
            jax.ShapeDtypeStruct((2 * HD, ROWS), BF16),
            jax.ShapeDtypeStruct((HALF, ROWS, 2 * HD), BF16),
            jax.ShapeDtypeStruct((HALF, ROWS, 2 * HD), BF16),
        ),
        in_specs=[SMEM, SMEM] + [VMEM] * 5 + [ANY] * BLOCKS,
        out_specs=(VMEM, VMEM, VMEM),
        scratch_shapes=[
            pltpu.VMEM((BLOCKS, PACKED, 2 * HD), BF16),
            pltpu.VMEM((2 * HD, ROWS), BF16),
            pltpu.VMEM((ROWS, 2 * HD), BF16),
            pltpu.VMEM((2, ROWS), F32),
            pltpu.VMEM((2 * HD, ROWS), F32),
            pltpu.SemaphoreType.DMA((BLOCKS,)),
        ],
    )(own, lowest, start, query, doutt, lse, out, *window)


def join_kernel(core_ref, mine_ref, got_ref, own_ref, *send_refs):
    core = core_ref[0]
    for d in range(HALF + 1):
        at = d - core
        inside = (at >= 0) & (at < HALF)
        other = got_ref[jnp.clip(at, 0, HALF - 1)].astype(F32)
        total = jnp.where(inside, other, 0.0)
        if d < HALF:
            total = total + mine_ref[d].astype(F32)
        if d == 0:
            own_ref[...] = total
        else:
            send_refs[d - 1][...] = total.astype(BF16)


def join_partials(core, mine, got):
    shape = (ROWS, 2 * HD)
    result = pl.pallas_call(
        join_kernel,
        name="join_partials",
        out_shape=(jax.ShapeDtypeStruct(shape, F32),) + (jax.ShapeDtypeStruct(shape, BF16),) * HALF,
        in_specs=[SMEM, VMEM, VMEM],
        out_specs=(VMEM,) * (HALF + 1),
    )(core, mine, got)
    return result[0], result[1:]


def total_kernel(own_ref, *refs):
    total = own_ref[...]
    for ref in refs[:HALF]:
        total = total + ref[...].astype(F32)
    refs[HALF][...] = total.astype(BF16).T


def total_partials(own, parts):
    return pl.pallas_call(
        total_kernel,
        name="total_partials",
        out_shape=jax.ShapeDtypeStruct((2 * HD, ROWS), BF16),
        in_specs=[VMEM] * (HALF + 1),
        out_specs=VMEM,
    )(own, *parts)


def project_kernel(deltas, at_ref, *refs):
    wq, wk, wv, pa, pb, gq, gkv, gq2, gkv2 = refs[:9]
    outs = refs[9 : 9 + len(deltas)]
    bq, bk, bv, bp, sem = refs[9 + len(deltas) :]
    z, xh, core = at_ref[0], at_ref[1], at_ref[2]
    copies = []
    for n, delta in enumerate(deltas):
        chunk = lax.rem(z + delta + RING, RING)
        rows = pl.ds(pl.multiple_of((2 * chunk + xh) * FEATS, 16), FEATS)
        mine = [
            pltpu.make_async_copy(w.at[rows, :], b.at[n], sem.at[n, i])
            for i, (w, b) in enumerate(((wq, bq), (wk, bk), (wv, bv)))
        ]
        for c in mine:
            c.start()
        half = lax.div(chunk, RING // 2)
        inner = lax.rem(chunk, RING // 2)

        @pl.when(half == core)
        def _(n=n, inner=inner):
            pltpu.make_async_copy(pa.at[inner], bp.at[n], sem.at[n, 3]).start()

        @pl.when(half != core)
        def _(n=n, inner=inner):
            pltpu.make_async_copy(pb.at[inner], bp.at[n], sem.at[n, 3]).start()

        copies.append(mine + [pltpu.make_async_copy(pa.at[0], bp.at[n], sem.at[n, 3])])
    for n in range(len(deltas)):
        for c in copies[n]:
            c.wait()
        total = dot(bq[n], gq[...]) + dot(bk[n], gkv[:HD, :]) + dot(bv[n], gkv[HD:, :])
        total = total + dot(bp[n, :, : 2 * HD], gq2[...]) + dot(bp[n, :, 2 * HD :], gkv2[...])
        outs[n][...] = total.astype(outs[n].dtype)


def project(deltas, at, weights, far, grads, kind):
    n = len(deltas)
    return pl.pallas_call(
        lambda *refs: project_kernel(deltas, *refs),
        name="project",
        out_shape=(jax.ShapeDtypeStruct((FEATS, ROWS), kind),) * n,
        in_specs=[SMEM] + [ANY] * 5 + [VMEM] * 4,
        out_specs=(VMEM,) * n,
        scratch_shapes=[
            pltpu.VMEM((n, FEATS, 2 * HD), BF16),
            pltpu.VMEM((n, FEATS, HD), BF16),
            pltpu.VMEM((n, FEATS, HD), BF16),
            pltpu.VMEM((n, FEATS, 4 * HD), BF16),
            pltpu.SemaphoreType.DMA((n, 4)),
        ],
    )(at, *weights, *far, *grads)


def swapped(x, axis):
    return lax.ppermute(x, axis, [(0, 1), (1, 0)])


def chip_pairs(d):
    return [(i, i + 2 * d) for i in range(lax.axis_size(AA) - 2 * d) if d < HALF or i % 2]


def chips_on(x, d):
    return lax.ppermute(x, AA, chip_pairs(d))


def chips_back(x, d):
    return lax.ppermute(x, AA, [(j, i) for i, j in chip_pairs(d)])


def round_z(x, step):
    return lax.ppermute(x, "z", [(i, (i + step) % RING) for i in range(RING)])


def local(query, keys, values, grad_out, segment_ids, w_query, w_key, w_value, w_out):
    core = lax.axis_index("core")
    z = lax.axis_index("z")
    xh = lax.axis_index("xh")
    own = lax.axis_index(AA)[None]
    at = jnp.stack((z, xh, core))
    ids = jnp.pad(
        segment_ids.astype(BF16).reshape(ROWS // HD, HD),
        ((0, SEG_ROWS - ROWS // HD), (0, HD)),
    )
    block = jnp.concatenate((jnp.concatenate((keys, values), axis=1), ids), axis=0)
    twins = [block] + [chips_on(block, d) for d in range(1, HALF + 1)]
    others = [
        swapped(jnp.where(core == 1, twins[d + 1], twins[d]), "core") for d in range(HALF)
    ]
    window = [None] * BLOCKS
    for d in range(HALF):
        window[BLOCKS - 1 - 2 * d] = twins[d]
        window[BLOCKS - 2 - 2 * d] = others[d]
    gathered = grad_out.T
    for axis in reversed(BA):
        gathered = lax.all_gather(gathered, axis, axis=0, tiled=True)
    wanted = [
        lax.dynamic_index_in_dim(w.reshape(2, RING // 2, 2, FEATS, -1), core, 0, keepdims=False)
        for w in (w_query, w_key, w_value)
    ]
    wanted = [lax.dynamic_index_in_dim(w, 1 - xh, 1, keepdims=False) for w in wanted]
    far_mine = swapped(jnp.concatenate(wanted, axis=2), "xh")
    far_other = swapped(far_mine, "core")

    stats = attention_stats(own, segment_ids[None, :], query, window)
    doutt = dot(w_out, gathered).astype(BF16)
    gqt, mine, theirs = attention_grads(own, stats, query, doutt, window)
    gqt_far = swapped(gqt, "xh")
    own_total, sends = join_partials(core[None], mine, swapped(theirs, "core"))
    parts = [chips_back(sends[d - 1], d) for d in range(HALF, 0, -1)]
    gkvt = total_partials(own_total, parts)
    gkvt_far = swapped(gkvt, "xh")

    weights = (w_query, w_key, w_value)
    far = (far_mine, far_other)
    grads = (gqt, gkvt, gqt_far, gkvt_far)
    ahead, behind = project((4, -3), at, weights, far, grads, BF16)
    rest = project((3, -2, 2, -1, 1, 0), at, weights, far, grads, F32)
    ahead = round_z(ahead, 1)
    behind = round_z(behind, -1)
    for add_ahead, add_behind in ((rest[0], rest[1]), (rest[2], rest[3])):
        ahead = round_z((ahead.astype(F32) + add_ahead).astype(BF16), 1)
        behind = round_z((behind.astype(F32) + add_behind).astype(BF16), -1)
    ahead = round_z((ahead.astype(F32) + rest[4]).astype(BF16), 1)
    result = (ahead.astype(F32) + behind.astype(F32) + rest[5]).astype(BF16)
    return result.T


def solution(mesh):
    finer = Mesh(mesh.devices.reshape(2, 4, 2, RING, 2), AA + BA)
    return jax.shard_map(
        local,
        mesh=finer,
        in_specs=(
            P(AA, BA),
            P(AA, BA),
            P(AA, BA),
            P(AA, BA),
            P(AA),
            P(None, BA),
            P(None, BA),
            P(None, BA),
            P(BA, None),
        ),
        out_specs=P(AA, BA),
        check_vma=False,
    )
```

time: 235 us -> 182 us (0.77); the launches traced: 234 us -> 179 us
  waiting for transfers between devices: 114 us -> 62.6 us
  Pallas kernels: 11.5 us -> 32.6 us
  starting transfers between devices: 49.9 us -> 39.3 us
  local copies, waits for them, and re-layouts: 12.8 us -> 3.64 us
  matrix products: 13.6 us -> 4.45 us
  other arithmetic: 4.72 us -> 10.6 us
    unnamed x5 -> x1, waiting for transfers between devices: 84 us -> 0.02 us
    pallas_call x2 -> x6, Pallas kernels: 11.5 us -> 32.6 us  [the longest x2 11.6 us: project(): pl.pallas_call(lambda *refs: project_kernel(deltas, *refs), name='project...]
    all_gather x1, waiting for transfers between devices: 1.14 us -> 18.6 us  [local(): gathered = lax.all_gather(gathered, axis, axis=0, tiled=True)]
    ppermute x18 -> x27, waiting for transfers between devices: 29.2 us -> 44 us  [the longest x5 15.9 us: chips_back(): return lax.ppermute(x, AA, [(j, i) for i, j in chip_pairs(d)])]
    dot_general x4 -> x1, matrix products: 13.6 us -> 4.45 us  [dot(): lax.dot_general(a, b, (((1,), (0,)), ((), ())), preferred_element_type=F32)]
    unnamed x20 -> x28, local copies, waits for them, and re-layouts: 8.09 us -> 0.74 us
    all_to_all x1 -> x0, starting transfers between devices: 6.69 us -> none  [sent_to_all(): return lax.all_to_all(copies, axis, split_axis=0, concat_axis=0, tiled=True)]
    ppermute x18 -> x27, starting transfers between devices: 43.2 us -> 39.3 us  [the longest x5 11.9 us: chips_on(): return lax.ppermute(x, AA, chip_pairs(d))]
  transfers between devices with their start and end apart: 22 -> 28, of which waited for: 14 -> 13; matrix products, arithmetic and copies ran while one was open for 4% -> 10% of each run, Pallas kernels for 2% -> 16%
where the time goes in v2:
time: 182 us; the launch traced here: 179 us
  waiting for transfers between devices  62.6 us (34%)
  starting transfers between devices  39.3 us (22%)
  Pallas kernels  32.6 us (18%)
  between operations  13.7 us (8%)
  blocking collectives  12.1 us (7%)
  other arithmetic  10.6 us (6%)
  matrix products  4.45 us (2%)
  local copies, waits for them, and re-layouts  3.64 us (2%)
    all_gather x1, waiting for transfers between devices, local(): gathered = lax.all_gather(gathered, axis, axis=0, tiled=True)  18.6 us
    ppermute x5, waiting for transfers between devices, chips_back(): return lax.ppermute(x, AA, [(j, i) for i, j in chip_pairs(d)])  15.9 us
    ppermute x7, waiting for transfers between devices, round_z(): return lax.ppermute(x, 'z', [(i, (i + step) % RING) for i in range(RING)])  15.2 us
    all_gather x1, blocking collectives, local(): gathered = lax.all_gather(gathered, axis, axis=0, tiled=True)  12.1 us
    ppermute x5, starting transfers between devices, chips_on(): return lax.ppermute(x, AA, chip_pairs(d))  11.9 us
    pallas_call x2, Pallas kernels, project(): pl.pallas_call(lambda *refs: project_kernel(deltas, *refs), name='project...  11.6 us
    ppermute x7, starting transfers between devices, round_z(): return lax.ppermute(x, 'z', [(i, (i + step) % RING) for i in range(RING)])  10.1 us
    ppermute x10, starting transfers between devices, swapped(): return lax.ppermute(x, axis, [(0, 1), (1, 0)])  9.32 us
  transfers between devices with their start and end apart: 28, of which 13 were waited for; matrix products, arithmetic and copies ran while one was open for 10% of the time, Pallas kernels for 16%

profile of v2, /device:TPU:24, one launch (start us, length us, event | category | flops | bytes accessed | tf_op | source)
XLA Modules:
  0.0 179.0 jit_solution(5615399185767434790)
XLA Ops:
  6.5 12.1 %all_gather.6 = bf16[672,384]{1,0:T(8,128)(2,1)} all-gather(bf16[336,384]{1,0:T(8,128)(2,1)} %bitcast.29), channel_id=1, replica_groups=mesh['xl'=2,'y'=4,'core'=2,'z'=8,'xh'=2] {'xh'}, dimensions={0}, use_global_device_ids=true | all-gather | bytes 774144 | tf_op jit(solution)/shard_map/all_gather | solution.py:341
  18.6 0.0 all-gather.2.cloned.1.call-update
  18.6 0.7 convert_bitcast_fusion
  19.3 1.6 fusion.2.refs_9_
  21.0 2.1 %collective-permute-start.9 = (bf16[400,256]{1,0:T(8,128)(2,1)}, bf16[400,256]{1,0:T(8,128)(2,1)S(1)}, u32[]{:S(2)}, u32[]{:S(2)}) collective-permute-start(bf16[400,256]{1,0:T(8,128)(2,1)} %fusion.2.refs_9_), channel_id=1, source_target_pairs={{0,32},{16,48},{32,64},{48,80},{64,96},{80,112},{96,128},{112,144}... | collective-permute-start | bytes 614408 | tf_op jit(solution)/shard_map/ppermute | solution.py:309
  23.1 4.5 %collective-permute-start.7 = (bf16[400,256]{1,0:T(8,128)(2,1)}, bf16[400,256]{1,0:T(8,128)(2,1)S(1)}, u32[]{:S(2)}, u32[]{:S(2)}) collective-permute-start(bf16[400,256]{1,0:T(8,128)(2,1)} %fusion.2.refs_9_), channel_id=1, source_target_pairs={{0,64},{16,80},{32,96},{48,112},{64,128},{80,144},{96,160},{112,17... | collective-permute-start | bytes 614408 | tf_op jit(solution)/shard_map/ppermute | solution.py:309
  27.6 1.9 %collective-permute-start.5 = (bf16[400,256]{1,0:T(8,128)(2,1)}, bf16[400,256]{1,0:T(8,128)(2,1)S(1)}, u32[]{:S(2)}, u32[]{:S(2)}) collective-permute-start(bf16[400,256]{1,0:T(8,128)(2,1)} %fusion.2.refs_9_), channel_id=1, source_target_pairs={{0,96},{16,112},{32,128},{48,144},{64,160},{80,176},{96,192},{112,... | collective-permute-start | bytes 614408 | tf_op jit(solution)/shard_map/ppermute | solution.py:309
  29.6 2.0 %collective-permute-start.3 = (bf16[400,256]{1,0:T(8,128)(2,1)}, bf16[400,256]{1,0:T(8,128)(2,1)}, u32[]{:S(2)}, u32[]{:S(2)}) collective-permute-start(bf16[400,256]{1,0:T(8,128)(2,1)} %fusion.2.refs_9_), channel_id=1, source_target_pairs={{0,128},{16,144},{32,160},{48,176},{64,192},{80,208},{96,224},{112... | collective-permute-start | bytes 614408 | tf_op jit(solution)/shard_map/ppermute | solution.py:309
  31.5 1.3 collective-permute-start.2
  32.9 1.2 dynamic-slice_bitcast_fusion
  34.0 1.1 dynamic-slice_bitcast_fusion.1
  35.2 0.0 copy-start.13
  35.2 1.2 pad_maximum_fusion
  36.4 0.0 collective-permute-done.9.refs_7_
  36.4 2.1 %collective-permute-start = (bf16[4,336,512]{2,1,0:T(8,128)(2,1)}, bf16[4,336,512]{2,1,0:T(8,128)(2,1)}, u32[]{:S(2)}, u32[]{:S(2)}) collective-permute-start(bf16[4,336,512]{2,1,0:T(8,128)(2,1)} %pad_maximum_fusion), channel_id=1, source_target_pairs={{0,1},{1,0},{2,3},{3,2},{4,5},{5,4},{6,7},{7,6},{8,9},{9,8},{10,11... | collective-permute-start | bytes 4128776 | tf_op jit(solution)/shard_map/ppermute | solution.py:301
  38.6 3.8 %collective-permute-done.3.refs_1_ = bf16[400,256]{1,0:T(8,128)(2,1)} collective-permute-done((bf16[400,256]{1,0:T(8,128)(2,1)}, bf16[400,256]{1,0:T(8,128)(2,1)}, u32[]{:S(2)}, u32[]{:S(2)}) %collective-permute-start.3) | collective-permute-done | bytes 204832 | tf_op jit(solution)/shard_map/ppermute | solution.py:309
  42.3 2.1 %broadcast_select_fusion = (bf16[400,256]{1,0:T(8,128)(2,1)S(1)}, bf16[400,256]{1,0:T(8,128)(2,1)}, bf16[400,256]{1,0:T(8,128)(2,1)}, bf16[400,256]{1,0:T(8,128)(2,1)}, bf16[400,256]{1,0:T(8,128)(2,1)}) fusion(bf16[400,256]{1,0:T(8,128)(2,1)S(1)} %collective-permute-done.9.refs_7_, pred[]{:T(512)S(6)} %eq.2, bf16[3,128]{1,0:T(4,128)(2,1)S(1)} %convert_bitcast_fusion, ...), kind=kLoop, calls=%fused_computation.15 | loop fusion | flops 1331200 | bytes 2245377 | tf_op jit(solution)/shard_map/jit(_where)/select_n | solution.py:333
  44.5 0.5 collective-permute-start.10
  45.0 0.5 collective-permute-start.6
  45.5 0.6 collective-permute-done.11.refs_8_
  46.0 0.1 collective-permute-start.4
  46.2 0.6 broadcast_in_dim.8.qseg_ref
  46.8 0.3 collective-permute-done.6.refs_2_
  47.1 0.8 collective-permute-done.4.refs_0_
  47.8 7.6 %attention_stats.1 = (f32[2,384]{1,0:T(2,128)}, f32[256,384]{1,0:T(8,128)}, s32[1,384]{1,0:T(1,128)}, s32[1]{0:T(128)}) custom-call(s32[1]{0:T(128)} %bitcast.9.own_ref, s32[1,384]{1,0:T(1,128)} %broadcast_in_dim.8.qseg_ref, bf16[384,256]{1,0:T(8,128)(2,1)} %q_ref.3, bf16[400,256]{1,0:T(8,128)(2,1)} %collective-permute-done.4.refs_0_, ...), custom_call_target="tpu_custom_call" | custom-call | tf_op jit(solution)/shard_map/attention_stats/pallas_call | solution.py:159
  55.5 18.6 %all-gather.2.cloned.1.call-done = bf16[5376,384]{1,0:T(8,128)(2,1)} async-done(((bf16[672,384]{1,0:T(8,128)(2,1)}), bf16[5376,384]{1,0:T(8,128)(2,1)}) %all-gather.2.cloned.1.call-update) | async-done | bytes 4128784 | tf_op jit(solution)/shard_map/all_gather | solution.py:341
  74.1 4.4 %convolution_convert_fusion.doutt_ref = bf16[256,384]{1,0:T(8,128)(2,1)} fusion(bf16[256,5376]{1,0:T(8,128)(2,1)S(1)} %copy-done, bf16[5376,384]{1,0:T(8,128)(2,1)} %all-gather.2.cloned.1.call-done), kind=kOutput, calls=%fused_computation.1 | convolution fusion | flops 1057062912 | bytes 7077888 | tf_op jit(solution)/shard_map/dot_general | solution.py:36
  78.6 8.5 %attention_grads.1 = (bf16[256,384]{1,0:T(8,128)(2,1)}, bf16[5,384,256]{2,1,0:T(8,128)(2,1)}, bf16[5,384,256]{2,1,0:T(8,128)(2,1)}) custom-call(s32[1]{0:T(128)} %bitcast.9.own_ref, s32[1]{0:T(128)} %get-tuple-element.26.low_ref, s32[1,384]{1,0:T(1,128)} %get-tuple-element.27.start_ref, bf16[384,256]{1,0:T(8,128)(2,1)} %q_ref.3, ...), custom_call_target="tpu_custom_call" | custom-call | tf_op jit(solution)/shard_map/attention_grads/pallas_call | solution.py:182
  87.0 0.1 collective-permute-start.12
  87.2 0.5 collective-permute-start.1
  87.7 2.4 %collective-permute-done.12.got_ref = bf16[5,384,256]{2,1,0:T(8,128)(2,1)} collective-permute-done((bf16[5,384,256]{2,1,0:T(8,128)(2,1)}, bf16[5,384,256]{2,1,0:T(8,128)(2,1)}, u32[]{:S(2)}, u32[]{:S(2)}) %collective-permute-start.12) | collective-permute-done | bytes 983072 | tf_op jit(solution)/shard_map/ppermute | solution.py:301
  90.0 2.6 %join_partials.1 = (f32[384,256]{1,0:T(8,128)}, bf16[384,256]{1,0:T(8,128)(2,1)}, bf16[384,256]{1,0:T(8,128)(2,1)}, bf16[384,256]{1,0:T(8,128)(2,1)}, bf16[384,2...) custom-call(s32[1]{0:T(128)} %bitcast.2.core_ref, bf16[5,384,256]{2,1,0:T(8,128)(2,1)} %get-tuple-element.31.mine_ref, ...), custom_call_target="tpu_custom_call" | custom-call | tf_op jit(solution)/shard_map/join_partials/pallas_call | solution.py:220
  92.7 0.7 collective-permute-start.13
  93.4 1.3 collective-permute-start.14
  94.7 1.9 %collective-permute-start.15 = (bf16[384,256]{1,0:T(8,128)(2,1)}, bf16[384,256]{1,0:T(8,128)(2,1)S(1)}, u32[]{:S(2)}, u32[]{:S(2)}) collective-permute-start(bf16[384,256]{1,0:T(8,128)(2,1)} %get-tuple-element.36), channel_id=1, source_target_pairs={{96,0},{112,16},{128,32},{144,48},{160,64},{176,80},{192,96},{208,... | collective-permute-start | bytes 589832 | tf_op jit(solution)/shard_map/ppermute | solution.py:313
  96.6 2.0 %collective-permute-start.16 = (bf16[384,256]{1,0:T(8,128)(2,1)}, bf16[384,256]{1,0:T(8,128)(2,1)}, u32[]{:S(2)}, u32[]{:S(2)}) collective-permute-start(bf16[384,256]{1,0:T(8,128)(2,1)} %get-tuple-element.37), channel_id=1, source_target_pairs={{64,0},{80,16},{96,32},{112,48},{128,64},{144,80},{160,96},{176,11... | collective-permute-start | bytes 589832 | tf_op jit(solution)/shard_map/ppermute | solution.py:313
  98.6 2.1 %collective-permute-start.17 = (bf16[384,256]{1,0:T(8,128)(2,1)}, bf16[384,256]{1,0:T(8,128)(2,1)}, u32[]{:S(2)}, u32[]{:S(2)}) collective-permute-start(bf16[384,256]{1,0:T(8,128)(2,1)} %get-tuple-element.38), channel_id=1, source_target_pairs={{32,0},{48,16},{64,32},{80,48},{96,64},{112,80},{128,96},{144,112}... | collective-permute-start | bytes 589832 | tf_op jit(solution)/shard_map/ppermute | solution.py:313
  100.7 7.2 %collective-permute-done.14.refs_1_ = bf16[384,256]{1,0:T(8,128)(2,1)S(1)} collective-permute-done((bf16[384,256]{1,0:T(8,128)(2,1)}, bf16[384,256]{1,0:T(8,128)(2,1)S(1)}, u32[]{:S(2)}, u32[]{:S(2)}) %collective-permute-start.14) | collective-permute-done | bytes 196640 | tf_op jit(solution)/shard_map/ppermute | solution.py:313
  108.0 2.7 %collective-permute-start.18 = (bf16[256,384]{1,0:T(8,128)(2,1)}, bf16[256,384]{1,0:T(8,128)(2,1)S(1)}, u32[]{:S(2)}, u32[]{:S(2)}) collective-permute-start(bf16[256,384]{1,0:T(8,128)(2,1)} %get-tuple-element.30.refs_6_), channel_id=1, source_target_pairs={{0,1},{1,0},{2,3},{3,2},{4,5},{5,4},{6,7},{7,6},{8,9},{9,8},{10,11... | collective-permute-start | bytes 589832 | tf_op jit(solution)/shard_map/ppermute | solution.py:301
  110.7 5.6 %collective-permute-done.16.refs_3_ = bf16[384,256]{1,0:T(8,128)(2,1)} collective-permute-done((bf16[384,256]{1,0:T(8,128)(2,1)}, bf16[384,256]{1,0:T(8,128)(2,1)}, u32[]{:S(2)}, u32[]{:S(2)}) %collective-permute-start.16) | collective-permute-done | bytes 196640 | tf_op jit(solution)/shard_map/ppermute | solution.py:313
  116.3 3.0 %collective-permute-done.17.refs_4_ = bf16[384,256]{1,0:T(8,128)(2,1)} collective-permute-done((bf16[384,256]{1,0:T(8,128)(2,1)}, bf16[384,256]{1,0:T(8,128)(2,1)}, u32[]{:S(2)}, u32[]{:S(2)}) %collective-permute-start.17) | collective-permute-done | bytes 196640 | tf_op jit(solution)/shard_map/ppermute | solution.py:313
  119.3 2.2 %total_partials.1.refs_7_ = bf16[256,384]{1,0:T(8,128)(2,1)} custom-call(f32[384,256]{1,0:T(8,128)} %get-tuple-element.33.own_ref, bf16[384,256]{1,0:T(8,128)(2,1)} %copy-done.10, bf16[384,256]{1,0:T(8,128)(2,1)} %copy-done.11, bf16[384,256]{1,0:T(8,128)(2,1)} %copy-done.12, bf16[384,256]{1,0:T(8,128)(2,1)} %collective-permute-done.16.refs_3_, ...), custom_call_target="tpu_custom_call" | custom-call | tf_op jit(solution)/shard_map/total_partials/pallas_call | solution.py:238
  121.5 2.8 %collective-permute-start.19 = (bf16[256,384]{1,0:T(8,128)(2,1)}, bf16[256,384]{1,0:T(8,128)(2,1)S(1)}, u32[]{:S(2)}, u32[]{:S(2)}) collective-permute-start(bf16[256,384]{1,0:T(8,128)(2,1)} %total_partials.1.refs_7_), channel_id=1, source_target_pairs={{0,1},{1,0},{2,3},{3,2},{4,5},{5,4},{6,7},{7,6},{8,9},{9,8},{10,11... | collective-permute-start | bytes 589832 | tf_op jit(solution)/shard_map/ppermute | solution.py:301
  124.3 0.6 pad_add_fusion.refs_0_
  124.9 5.1 %collective-permute-done.19.refs_9_ = bf16[256,384]{1,0:T(8,128)(2,1)S(1)} collective-permute-done((bf16[256,384]{1,0:T(8,128)(2,1)}, bf16[256,384]{1,0:T(8,128)(2,1)S(1)}, u32[]{:S(2)}, u32[]{:S(2)}) %collective-permute-start.19) | collective-permute-done | bytes 196640 | tf_op jit(solution)/shard_map/ppermute | solution.py:301
  130.0 0.7 copy-done.5
  130.7 4.3 %project.2 = (bf16[336,384]{1,0:T(8,128)(2,1)}, bf16[336,384]{1,0:T(8,128)(2,1)}) custom-call(s32[3]{0:T(128)} %pad_add_fusion.refs_0_, bf16[5376,256]{1,0:T(8,128)(2,1)} %refs_1_.3, bf16[5376,128]{1,0:T(8,128)(2,1)} %refs_2_.3, bf16[5376,128]{1,0:T(8,128)(2,1)} %refs_3_.3, bf16[4,336,512]{2,1,0:T(8,128)(2,1)} %collective-permute-done.refs_4_, ...), custom_call_target="tpu_custom_call" | custom-call | tf_op jit(solution)/shard_map/project/pallas_call | solution.py:284
  135.1 0.1 collective-permute-start.20
  135.2 3.2 %collective-permute-start.24 = (bf16[336,384]{1,0:T(8,128)(2,1)}, bf16[336,384]{1,0:T(8,128)(2,1)S(1)}, u32[]{:S(2)}, u32[]{:S(2)}) collective-permute-start(bf16[336,384]{1,0:T(8,128)(2,1)} %get-tuple-element.43), channel_id=1, source_target_pairs={{0,14},{2,0},{4,2},{6,4},{8,6},{10,8},{12,10},{14,12},{1,15},{3,1}... | collective-permute-start | bytes 774152 | tf_op jit(solution)/shard_map/ppermute | solution.py:317
  138.4 7.3 %project.3 = (f32[336,384]{1,0:T(8,128)}, f32[336,384]{1,0:T(8,128)}, f32[336,384]{1,0:T(8,128)}, f32[336,384]{1,0:T(8,128)}, f32[336,384]{1,0:T(8,128)}, /*index=5*/f32[336,384]{1,0:T(8,128)}) custom-call(s32[3]{0:T(128)} %pad_add_fusion.refs_0_, bf16[5376,256]{1,0:T(8,128)(2,1)} %refs_1_.3, bf16[5376,128]{1,0:T(8,128)(2,1)} %refs_2_.3, ...), custom_call_target="tpu_custom_call" | custom-call | tf_op jit(solution)/shard_map/project/pallas_call | solution.py:284
  145.7 1.2 add_convert_fusion.5
  146.9 0.1 collective-permute-start.21
  147.0 1.1 add_convert_fusion.2
  148.1 3.3 %collective-permute-start.25 = (bf16[336,384]{1,0:T(8,128)(2,1)S(1)}, bf16[336,384]{1,0:T(8,128)(2,1)S(1)}, u32[]{:S(2)}, u32[]{:S(2)}) collective-permute-start(bf16[336,384]{1,0:T(8,128)(2,1)S(1)} %add_convert_fusion.2), channel_id=1, source_target_pairs={{0,14},{2,0},{4,2},{6,4},{8,6},{10,8},{12,10},{14,12},{1,15},{3,1}... | collective-permute-start | bytes 774152 | tf_op jit(solution)/shard_map/ppermute | solution.py:317
  151.4 3.5 %collective-permute-done.21 = bf16[336,384]{1,0:T(8,128)(2,1)S(1)} collective-permute-done((bf16[336,384]{1,0:T(8,128)(2,1)S(1)}, bf16[336,384]{1,0:T(8,128)(2,1)S(1)}, u32[]{:S(2)}, u32[]{:S(2)}) %collective-permute-start.21) | collective-permute-done | bytes 258080 | tf_op jit(solution)/shard_map/ppermute | solution.py:317
  154.9 1.1 add_convert_fusion.4
  156.0 0.1 collective-permute-start.22
  156.1 0.1 add_convert_fusion.1
  156.2 3.3 %collective-permute-start.26 = (bf16[336,384]{1,0:T(8,128)(2,1)S(1)}, bf16[336,384]{1,0:T(8,128)(2,1)S(1)}, u32[]{:S(2)}, u32[]{:S(2)}) collective-permute-start(bf16[336,384]{1,0:T(8,128)(2,1)S(1)} %add_convert_fusion.1), channel_id=1, source_target_pairs={{0,14},{2,0},{4,2},{6,4},{8,6},{10,8},{12,10},{14,12},{1,15},{3,1}... | collective-permute-start | bytes 774152 | tf_op jit(solution)/shard_map/ppermute | solution.py:317
  159.5 4.2 %collective-permute-done.22 = bf16[336,384]{1,0:T(8,128)(2,1)S(1)} collective-permute-done((bf16[336,384]{1,0:T(8,128)(2,1)S(1)}, bf16[336,384]{1,0:T(8,128)(2,1)S(1)}, u32[]{:S(2)}, u32[]{:S(2)}) %collective-permute-start.22) | collective-permute-done | bytes 258080 | tf_op jit(solution)/shard_map/ppermute | solution.py:317
  163.6 0.1 add_convert_fusion.3
  163.7 0.1 collective-permute-start.23
  163.8 7.5 %collective-permute-done.23 = bf16[336,384]{1,0:T(8,128)(2,1)S(1)} collective-permute-done((bf16[336,384]{1,0:T(8,128)(2,1)S(1)}, bf16[336,384]{1,0:T(8,128)(2,1)S(1)}, u32[]{:S(2)}, u32[]{:S(2)}) %collective-permute-start.23) | collective-permute-done | bytes 258080 | tf_op jit(solution)/shard_map/ppermute | solution.py:317
  171.3 0.8 fusion.1
  (43 shorter events, 0.1 us)
Async XLA Ops:
  6.5 67.6 %copy-start = (bf16[256,5376]{1,0:T(8,128)(2,1)S(1)}, bf16[256,5376]{1,0:T(8,128)(2,1)}, u32[]{:S(2)}) copy-start(bf16[256,5376]{1,0:T(8,128)(2,1)} %param.17) | copy-start | bytes 8257540
  6.5 67.6 %all-gather.2.cloned.1.call-start = ((), (), s32[]{:S(2)}) async-start(), calls=%async_computation | async-start | bytes 4644864 | tf_op jit(solution)/shard_map/all_gather | solution.py:341
  21.0 15.5 %collective-permute-start.9 = (bf16[400,256]{1,0:T(8,128)(2,1)}, bf16[400,256]{1,0:T(8,128)(2,1)S(1)}, u32[]{:S(2)}, u32[]{:S(2)}) collective-permute-start(bf16[400,256]{1,0:T(8,128)(2,1)} %fusion.2.refs_9_), channel_id=1, source_target_pairs={{0,32},{16,48},{32,64},{48,80},{64,96},{80,112},{96,128},{112,144}... | collective-permute-start | bytes 614408 | tf_op jit(solution)/shard_map/ppermute | solution.py:309
  23.1 15.4 %collective-permute-start.7 = (bf16[400,256]{1,0:T(8,128)(2,1)}, bf16[400,256]{1,0:T(8,128)(2,1)S(1)}, u32[]{:S(2)}, u32[]{:S(2)}) collective-permute-start(bf16[400,256]{1,0:T(8,128)(2,1)} %fusion.2.refs_9_), channel_id=1, source_target_pairs={{0,64},{16,80},{32,96},{48,112},{64,128},{80,144},{96,160},{112,17... | collective-permute-start | bytes 614408 | tf_op jit(solution)/shard_map/ppermute | solution.py:309
  27.6 10.9 %collective-permute-start.5 = (bf16[400,256]{1,0:T(8,128)(2,1)}, bf16[400,256]{1,0:T(8,128)(2,1)S(1)}, u32[]{:S(2)}, u32[]{:S(2)}) collective-permute-start(bf16[400,256]{1,0:T(8,128)(2,1)} %fusion.2.refs_9_), channel_id=1, source_target_pairs={{0,96},{16,112},{32,128},{48,144},{64,160},{80,176},{96,192},{112,... | collective-permute-start | bytes 614408 | tf_op jit(solution)/shard_map/ppermute | solution.py:309
  29.6 12.8 %collective-permute-start.3 = (bf16[400,256]{1,0:T(8,128)(2,1)}, bf16[400,256]{1,0:T(8,128)(2,1)}, u32[]{:S(2)}, u32[]{:S(2)}) collective-permute-start(bf16[400,256]{1,0:T(8,128)(2,1)} %fusion.2.refs_9_), channel_id=1, source_target_pairs={{0,128},{16,144},{32,160},{48,176},{64,192},{80,208},{96,224},{112... | collective-permute-start | bytes 614408 | tf_op jit(solution)/shard_map/ppermute | solution.py:309
  31.5 10.8 %collective-permute-start.2 = (bf16[400,256]{1,0:T(8,128)(2,1)}, bf16[400,256]{1,0:T(8,128)(2,1)}, u32[]{:S(2)}, u32[]{:S(2)}) collective-permute-start(bf16[400,256]{1,0:T(8,128)(2,1)} %fusion.2.refs_9_), channel_id=1, source_target_pairs={{16,176},{48,208},{80,240},{17,177},{49,209},{81,241},{18,178},{50... | collective-permute-start | bytes 614408 | tf_op jit(solution)/shard_map/ppermute | solution.py:309
  32.9 9.5 %copy-start.9 = (bf16[384,128]{1,0:T(8,128)(2,1)S(1)}, bf16[384,128]{1,0:T(8,128)(2,1)}, u32[]{:S(2)}) copy-start(bf16[384,128]{1,0:T(8,128)(2,1)} %param.11) | copy-start | bytes 294916
  35.2 11.0 %copy-start.13 = (s32[384]{0:T(512)S(1)}, s32[384]{0:T(512)}, u32[]{:S(2)}) copy-start(s32[384]{0:T(512)} %param.13) | copy-start | bytes 4612
  36.4 11.4 %copy-start.1 = (bf16[400,256]{1,0:T(8,128)(2,1)}, bf16[400,256]{1,0:T(8,128)(2,1)S(1)}, u32[]{:S(2)}) copy-start(bf16[400,256]{1,0:T(8,128)(2,1)S(1)} %collective-permute-done.9.refs_7_) | copy-start | bytes 614404
  36.4 50.7 %collective-permute-start = (bf16[4,336,512]{2,1,0:T(8,128)(2,1)}, bf16[4,336,512]{2,1,0:T(8,128)(2,1)}, u32[]{:S(2)}, u32[]{:S(2)}) collective-permute-start(bf16[4,336,512]{2,1,0:T(8,128)(2,1)} %pad_maximum_fusion), channel_id=1, source_target_pairs={{0,1},{1,0},{2,3},{3,2},{4,5},{5,4},{6,7},{7,6},{8,9},{9,8},{10,11... | collective-permute-start | bytes 4128776 | tf_op jit(solution)/shard_map/ppermute | solution.py:301
  38.5 9.3 %copy-start.2 = (bf16[400,256]{1,0:T(8,128)(2,1)}, bf16[400,256]{1,0:T(8,128)(2,1)S(1)}, u32[]{:S(2)}) copy-start(bf16[400,256]{1,0:T(8,128)(2,1)S(1)} %collective-permute-done.7.refs_5_) | copy-start | bytes 614404
  38.6 9.3 %copy-start.3 = (bf16[400,256]{1,0:T(8,128)(2,1)}, bf16[400,256]{1,0:T(8,128)(2,1)S(1)}, u32[]{:S(2)}) copy-start(bf16[400,256]{1,0:T(8,128)(2,1)S(1)} %collective-permute-done.5.refs_3_) | copy-start | bytes 614404
  44.5 1.6 collective-permute-start.11
  44.5 2.3 %collective-permute-start.10 = (bf16[400,256]{1,0:T(8,128)(2,1)}, bf16[400,256]{1,0:T(8,128)(2,1)}, u32[]{:S(2)}, u32[]{:S(2)}) collective-permute-start(bf16[400,256]{1,0:T(8,128)(2,1)} %get-tuple-element.48), channel_id=1, source_target_pairs={{0,16},{16,0},{1,17},{17,1},{2,18},{18,2},{3,19},{19,3},{4,20},{20... | collective-permute-start | bytes 614408 | tf_op jit(solution)/shard_map/ppermute | solution.py:301
  45.0 1.8 %collective-permute-start.8 = (bf16[400,256]{1,0:T(8,128)(2,1)}, bf16[400,256]{1,0:T(8,128)(2,1)}, u32[]{:S(2)}, u32[]{:S(2)}) collective-permute-start(bf16[400,256]{1,0:T(8,128)(2,1)} %get-tuple-element.49), channel_id=1, source_target_pairs={{0,16},{16,0},{1,17},{17,1},{2,18},{18,2},{3,19},{19,3},{4,20},{20... | collective-permute-start | bytes 614408 | tf_op jit(solution)/shard_map/ppermute | solution.py:301
  45.0 2.1 %collective-permute-start.6 = (bf16[400,256]{1,0:T(8,128)(2,1)}, bf16[400,256]{1,0:T(8,128)(2,1)}, u32[]{:S(2)}, u32[]{:S(2)}) collective-permute-start(bf16[400,256]{1,0:T(8,128)(2,1)} %get-tuple-element.50), channel_id=1, source_target_pairs={{0,16},{16,0},{1,17},{17,1},{2,18},{18,2},{3,19},{19,3},{4,20},{20... | collective-permute-start | bytes 614408 | tf_op jit(solution)/shard_map/ppermute | solution.py:301
  46.0 1.8 %collective-permute-start.4 = (bf16[400,256]{1,0:T(8,128)(2,1)}, bf16[400,256]{1,0:T(8,128)(2,1)}, u32[]{:S(2)}, u32[]{:S(2)}) collective-permute-start(bf16[400,256]{1,0:T(8,128)(2,1)} %get-tuple-element.51), channel_id=1, source_target_pairs={{0,16},{16,0},{1,17},{17,1},{2,18},{18,2},{3,19},{19,3},{4,20},{20... | collective-permute-start | bytes 614408 | tf_op jit(solution)/shard_map/ppermute | solution.py:301
  87.0 3.0 %collective-permute-start.12 = (bf16[5,384,256]{2,1,0:T(8,128)(2,1)}, bf16[5,384,256]{2,1,0:T(8,128)(2,1)}, u32[]{:S(2)}, u32[]{:S(2)}) collective-permute-start(bf16[5,384,256]{2,1,0:T(8,128)(2,1)} %get-tuple-element.32), channel_id=1, source_target_pairs={{0,16},{16,0},{1,17},{17,1},{2,18},{18,2},{3,19},{19,3},{4,20},{20... | collective-permute-start | bytes 2949128 | tf_op jit(solution)/shard_map/ppermute | solution.py:301
  87.2 37.8 %collective-permute-start.1 = (bf16[4,336,512]{2,1,0:T(8,128)(2,1)}, bf16[4,336,512]{2,1,0:T(8,128)(2,1)}, u32[]{:S(2)}, u32[]{:S(2)}) collective-permute-start(bf16[4,336,512]{2,1,0:T(8,128)(2,1)} %collective-permute-done.refs_4_), channel_id=1, source_target_pairs={{0,16},{16,0},{1,17},{17,1},{2,18},{18,2},{3,19},{19,3},{4,20},{20... | collective-permute-start | bytes 4128776 | tf_op jit(solution)/shard_map/ppermute | solution.py:301
  92.7 5.9 %collective-permute-start.13 = (bf16[384,256]{1,0:T(8,128)(2,1)}, bf16[384,256]{1,0:T(8,128)(2,1)S(1)}, u32[]{:S(2)}, u32[]{:S(2)}) collective-permute-start(bf16[384,256]{1,0:T(8,128)(2,1)} %get-tuple-element.34), channel_id=1, source_target_pairs={{176,16},{208,48},{240,80},{177,17},{209,49},{241,81},{178,18},{21... | collective-permute-start | bytes 589832 | tf_op jit(solution)/shard_map/ppermute | solution.py:313
  93.4 14.6 %collective-permute-start.14 = (bf16[384,256]{1,0:T(8,128)(2,1)}, bf16[384,256]{1,0:T(8,128)(2,1)S(1)}, u32[]{:S(2)}, u32[]{:S(2)}) collective-permute-start(bf16[384,256]{1,0:T(8,128)(2,1)} %get-tuple-element.35), channel_id=1, source_target_pairs={{128,0},{144,16},{160,32},{176,48},{192,64},{208,80},{224,96},{240... | collective-permute-start | bytes 589832 | tf_op jit(solution)/shard_map/ppermute | solution.py:313
  94.7 16.0 %collective-permute-start.15 = (bf16[384,256]{1,0:T(8,128)(2,1)}, bf16[384,256]{1,0:T(8,128)(2,1)S(1)}, u32[]{:S(2)}, u32[]{:S(2)}) collective-permute-start(bf16[384,256]{1,0:T(8,128)(2,1)} %get-tuple-element.36), channel_id=1, source_target_pairs={{96,0},{112,16},{128,32},{144,48},{160,64},{176,80},{192,96},{208,... | collective-permute-start | bytes 589832 | tf_op jit(solution)/shard_map/ppermute | solution.py:313
  96.6 19.7 %collective-permute-start.16 = (bf16[384,256]{1,0:T(8,128)(2,1)}, bf16[384,256]{1,0:T(8,128)(2,1)}, u32[]{:S(2)}, u32[]{:S(2)}) collective-permute-start(bf16[384,256]{1,0:T(8,128)(2,1)} %get-tuple-element.37), channel_id=1, source_target_pairs={{64,0},{80,16},{96,32},{112,48},{128,64},{144,80},{160,96},{176,11... | collective-permute-start | bytes 589832 | tf_op jit(solution)/shard_map/ppermute | solution.py:313
  98.6 20.7 %copy-start.10 = (bf16[384,256]{1,0:T(8,128)(2,1)}, bf16[384,256]{1,0:T(8,128)(2,1)S(1)}, u32[]{:S(2)}) copy-start(bf16[384,256]{1,0:T(8,128)(2,1)S(1)} %collective-permute-done.13.refs_0_) | copy-start | bytes 589828
  98.6 20.7 %collective-permute-start.17 = (bf16[384,256]{1,0:T(8,128)(2,1)}, bf16[384,256]{1,0:T(8,128)(2,1)}, u32[]{:S(2)}, u32[]{:S(2)}) collective-permute-start(bf16[384,256]{1,0:T(8,128)(2,1)} %get-tuple-element.38), channel_id=1, source_target_pairs={{32,0},{48,16},{64,32},{80,48},{96,64},{112,80},{128,96},{144,112}... | collective-permute-start | bytes 589832 | tf_op jit(solution)/shard_map/ppermute | solution.py:313
  108.0 11.3 %copy-start.11 = (bf16[384,256]{1,0:T(8,128)(2,1)}, bf16[384,256]{1,0:T(8,128)(2,1)S(1)}, u32[]{:S(2)}) copy-start(bf16[384,256]{1,0:T(8,128)(2,1)S(1)} %collective-permute-done.14.refs_1_) | copy-start | bytes 589828
  108.0 17.0 %collective-permute-start.18 = (bf16[256,384]{1,0:T(8,128)(2,1)}, bf16[256,384]{1,0:T(8,128)(2,1)S(1)}, u32[]{:S(2)}, u32[]{:S(2)}) collective-permute-start(bf16[256,384]{1,0:T(8,128)(2,1)} %get-tuple-element.30.refs_6_), channel_id=1, source_target_pairs={{0,1},{1,0},{2,3},{3,2},{4,5},{5,4},{6,7},{7,6},{8,9},{9,8},{10,11... | collective-permute-start | bytes 589832 | tf_op jit(solution)/shard_map/ppermute | solution.py:301
  110.6 8.6 %copy-start.12 = (bf16[384,256]{1,0:T(8,128)(2,1)}, bf16[384,256]{1,0:T(8,128)(2,1)S(1)}, u32[]{:S(2)}) copy-start(bf16[384,256]{1,0:T(8,128)(2,1)S(1)} %collective-permute-done.15.refs_2_) | copy-start | bytes 589828
  121.5 8.5 %collective-permute-start.19 = (bf16[256,384]{1,0:T(8,128)(2,1)}, bf16[256,384]{1,0:T(8,128)(2,1)S(1)}, u32[]{:S(2)}, u32[]{:S(2)}) collective-permute-start(bf16[256,384]{1,0:T(8,128)(2,1)} %total_partials.1.refs_7_), channel_id=1, source_target_pairs={{0,1},{1,0},{2,3},{3,2},{4,5},{5,4},{6,7},{7,6},{8,9},{9,8},{10,11... | collective-permute-start | bytes 589832 | tf_op jit(solution)/shard_map/ppermute | solution.py:301
  124.9 5.1 %copy-start.4 = (bf16[256,384]{1,0:T(8,128)(2,1)}, bf16[256,384]{1,0:T(8,128)(2,1)S(1)}, u32[]{:S(2)}) copy-start(bf16[256,384]{1,0:T(8,128)(2,1)S(1)} %collective-permute-done.18.refs_8_) | copy-start | bytes 589828
  130.0 0.7 copy-start.5
  135.1 10.6 %collective-permute-start.20 = (bf16[336,384]{1,0:T(8,128)(2,1)}, bf16[336,384]{1,0:T(8,128)(2,1)S(1)}, u32[]{:S(2)}, u32[]{:S(2)}) collective-permute-start(bf16[336,384]{1,0:T(8,128)(2,1)} %get-tuple-element.39), channel_id=1, source_target_pairs={{0,2},{2,4},{4,6},{6,8},{8,10},{10,12},{12,14},{14,0},{1,3},{3,5},... | collective-permute-start | bytes 774152 | tf_op jit(solution)/shard_map/ppermute | solution.py:317
  135.2 11.8 %collective-permute-start.24 = (bf16[336,384]{1,0:T(8,128)(2,1)}, bf16[336,384]{1,0:T(8,128)(2,1)S(1)}, u32[]{:S(2)}, u32[]{:S(2)}) collective-permute-start(bf16[336,384]{1,0:T(8,128)(2,1)} %get-tuple-element.43), channel_id=1, source_target_pairs={{0,14},{2,0},{4,2},{6,4},{8,6},{10,8},{12,10},{14,12},{1,15},{3,1}... | collective-permute-start | bytes 774152 | tf_op jit(solution)/shard_map/ppermute | solution.py:317
  145.7 10.5 %copy-start.8 = (f32[336,384]{1,0:T(8,128)S(1)}, f32[336,384]{1,0:T(8,128)}, u32[]{:S(2)}) copy-start(f32[336,384]{1,0:T(8,128)} %get-tuple-element.45) | copy-start | bytes 1548292
  145.7 18.0 %copy-start.7 = (f32[336,384]{1,0:T(8,128)S(1)}, f32[336,384]{1,0:T(8,128)}, u32[]{:S(2)}) copy-start(f32[336,384]{1,0:T(8,128)} %get-tuple-element.42) | copy-start | bytes 1548292
  145.7 25.6 %copy-start.6 = (f32[336,384]{1,0:T(8,128)S(1)}, f32[336,384]{1,0:T(8,128)}, u32[]{:S(2)}) copy-start(f32[336,384]{1,0:T(8,128)} %get-tuple-element.46) | copy-start | bytes 1548292
  146.9 8.0 %collective-permute-start.21 = (bf16[336,384]{1,0:T(8,128)(2,1)S(1)}, bf16[336,384]{1,0:T(8,128)(2,1)S(1)}, u32[]{:S(2)}, u32[]{:S(2)}) collective-permute-start(bf16[336,384]{1,0:T(8,128)(2,1)S(1)} %add_convert_fusion.5), channel_id=1, source_target_pairs={{0,2},{2,4},{4,6},{6,8},{8,10},{10,12},{12,14},{14,0},{1,3},{3,5},... | collective-permute-start | bytes 774152 | tf_op jit(solution)/shard_map/ppermute | solution.py:317
  148.1 8.0 %collective-permute-start.25 = (bf16[336,384]{1,0:T(8,128)(2,1)S(1)}, bf16[336,384]{1,0:T(8,128)(2,1)S(1)}, u32[]{:S(2)}, u32[]{:S(2)}) collective-permute-start(bf16[336,384]{1,0:T(8,128)(2,1)S(1)} %add_convert_fusion.2), channel_id=1, source_target_pairs={{0,14},{2,0},{4,2},{6,4},{8,6},{10,8},{12,10},{14,12},{1,15},{3,1}... | collective-permute-start | bytes 774152 | tf_op jit(solution)/shard_map/ppermute | solution.py:317
  156.0 7.6 %collective-permute-start.22 = (bf16[336,384]{1,0:T(8,128)(2,1)S(1)}, bf16[336,384]{1,0:T(8,128)(2,1)S(1)}, u32[]{:S(2)}, u32[]{:S(2)}) collective-permute-start(bf16[336,384]{1,0:T(8,128)(2,1)S(1)} %add_convert_fusion.4), channel_id=1, source_target_pairs={{0,2},{2,4},{4,6},{6,8},{8,10},{10,12},{12,14},{14,0},{1,3},{3,5},... | collective-permute-start | bytes 774152 | tf_op jit(solution)/shard_map/ppermute | solution.py:317
  156.2 7.6 %collective-permute-start.26 = (bf16[336,384]{1,0:T(8,128)(2,1)S(1)}, bf16[336,384]{1,0:T(8,128)(2,1)S(1)}, u32[]{:S(2)}, u32[]{:S(2)}) collective-permute-start(bf16[336,384]{1,0:T(8,128)(2,1)S(1)} %add_convert_fusion.1), channel_id=1, source_target_pairs={{0,14},{2,0},{4,2},{6,4},{8,6},{10,8},{12,10},{14,12},{1,15},{3,1}... | collective-permute-start | bytes 774152 | tf_op jit(solution)/shard_map/ppermute | solution.py:317
  163.7 7.6 %collective-permute-start.23 = (bf16[336,384]{1,0:T(8,128)(2,1)S(1)}, bf16[336,384]{1,0:T(8,128)(2,1)S(1)}, u32[]{:S(2)}, u32[]{:S(2)}) collective-permute-start(bf16[336,384]{1,0:T(8,128)(2,1)S(1)} %add_convert_fusion.3), channel_id=1, source_target_pairs={{0,2},{2,4},{4,6},{6,8},{8,10},{10,12},{12,14},{14,0},{1,3},{3,5},... | collective-permute-start | bytes 774152 | tf_op jit(solution)/shard_map/ppermute | solution.py:317
Sparse Core Ops, SparseCore 0:
  18.8 55.3 all-gather.1
